TPU v7x, 128 devices: a whole 4x4x4 slice. The times are simulated.
128 devices in a mesh: win: 16 (over y, x_hi, core), tile: 8 (over x_lo, z).
Axes of the slice: x: 4 (x_hi: 2, x_lo: 2; x = x_hi * 2 + x_lo), y: 4, z: 4, core: 2. Of those that a mesh axis runs over, the one named last changes fastest.
Arguments:
- flux: bfloat16 [3840, 65536], P('win', 'tile'), may hold values from -6 to 6
- prior_std: float32 [3840, 65536], P('win', 'tile'), may hold values from 0.3 to 3
- footprint: bfloat16 [16384, 128, 128], P('win', 'tile'), may hold values from 0.0099487305 to 1
- obs_value: float32 [16384], P('win'), may hold values from -180 to 180
- obs_weight: float32 [16384], P('win'), may hold values from 0.002 to 0.02
- obs_hour: int32 [16384], P('win'), may hold values from 0 to 239
- hour_offset: int32 [16384, 128], P('win', 'tile'), may hold values from 0 to 239
- block_cell: int32 [16384, 128], P('win', 'tile'), may hold values from 0 to 63
Outputs:
- gradient: float32 [3840, 65536], P('win', 'tile')
Inputs may be any that keep to these rules, and one draw needn't show every extreme that they name: `block_cell`: index of a block of 128 cells within the tile.
All inputs are finite; a program needn't handle non-finite values.
Results may differ from a plain program's by a relative error of at most 0.0003.
Values may be sent and summed in bfloat16 or wider, within the bound.
A program may use at most 128 MiB of HBM per device.

v0:
```python
import jax
import jax.numpy as jnp
from jax import lax
from jax.sharding import PartitionSpec as P

KH = 24


def from_behind(value, axis, steps):
    count = lax.axis_size(axis)
    initial, last = (max(0, -steps), min(count, count - steps))
    return lax.ppermute(value, axis, [(source, source + steps) for source in range(initial, last)])


def extended(cells, sides, width):
    for axis, dim in sides:
        count = lax.axis_size(axis)
        ends = count - 1
        head = lax.slice_in_dim(cells, 0, width, axis=dim)
        tail = lax.slice_in_dim(cells, cells.shape[dim] - width, cells.shape[dim], axis=dim)
        cells = jnp.concatenate(
            [
                lax.ppermute(tail, axis, [(i, (i + 1) % count) for i in range(ends)]),
                cells,
                lax.ppermute(head, axis, [((i + 1) % count, i) for i in range(ends)]),
            ],
            axis=dim,
        )
    return cells


def misfits(partial_value, obs_value, obs_weight):
    predicted = lax.psum(partial_value, "tile")
    return (predicted - obs_value) * obs_weight


def shards(flux, prior_std, footprint, obs_value, obs_weight, obs_hour, hour_offset, block_cell):
    hours = flux.shape[0]
    cells = flux.shape[1]
    width = footprint.shape[2]
    per_hour = cells // width
    earlier = from_behind(flux, "win", 1)
    joined = jnp.concatenate([earlier, flux], axis=0).reshape(2 * hours * per_hour, width)
    flat = (hours + obs_hour[:, None] - hour_offset) * per_hour + block_cell
    picked = joined[flat]
    partial_value = jnp.einsum("onc,onc->o", footprint, picked, preferred_element_type=jnp.float32)
    weighted = misfits(partial_value, obs_value, obs_weight)
    contrib = weighted[:, None, None] * footprint.astype(jnp.float32)
    summed = jax.ops.segment_sum(
        contrib.reshape(-1, width), flat.reshape(-1), num_segments=2 * hours * per_hour
    )
    summed = summed.reshape(2 * hours, cells)
    returned = from_behind(summed[:hours], "win", -1)
    adjoint = summed[hours:] + returned
    scaled = prior_std * adjoint
    rim = extended(scaled, (("win", 0),), KH)
    rows = jnp.arange(hours, dtype=jnp.int32)[:, None]
    columns = jnp.arange(hours + 2 * KH, dtype=jnp.int32)[None, :]
    distance = columns - rows - KH
    kernel = jnp.where(
        jnp.abs(distance) <= KH, jnp.exp(-2.0 * jnp.abs(distance).astype(jnp.float32) / KH), 0.0
    )
    smoothed = jnp.dot(
        kernel, rim, preferred_element_type=jnp.float32, precision=lax.Precision.HIGHEST
    )
    return prior_std * smoothed


def solution(mesh):
    return jax.shard_map(
        shards,
        mesh=mesh,
        in_specs=(
            P("win", "tile"),
            P("win", "tile"),
            P("win", "tile", None),
            P("win"),
            P("win"),
            P("win"),
            P("win", "tile"),
            P("win", "tile"),
        ),
        out_specs=P("win", "tile"),
        check_vma=False,
    )
```

profile of v0, /device:TPU:1, one launch (start us, length us, event | category | flops | bytes accessed | tf_op | source)
XLA Modules:
  0.0 422.3 jit_solution(7322653680704926286)
XLA Ops:
  0.0 6.0 %collective-permute-start = (bf16[240,8192]{1,0:T(8,128)(2,1)}, bf16[240,8192]{1,0:T(8,128)(2,1)}, u32[]{:S(2)}, u32[]{:S(2)}) collective-permute-start(bf16[240,8192]{1,0:T(8,128)(2,1)} %param.8), channel_id=1, source_target_pairs={{0,8},{8,16},{16,24},{24,32},{32,40},{40,48},{48,56},{56,64},{64,7... | collective-permute-start | bytes 11796488 | tf_op jit(solution)/shard_map/ppermute | solution.py:12
  6.0 0.7 broadcast_add_fusion
  6.7 0.9 compare_select_fusion
  7.6 0.2 copy.10
  7.8 0.2 reshape.16
  8.0 0.2 copy.9
  8.2 0.2 reshape.24
  8.4 40.5 %collective-permute-done = bf16[240,8192]{1,0:T(8,128)(2,1)} collective-permute-done((bf16[240,8192]{1,0:T(8,128)(2,1)}, bf16[240,8192]{1,0:T(8,128)(2,1)}, u32[]{:S(2)}, u32[]{:S(2)}) %collective-permute-start) | collective-permute-done | bytes 3932192 | tf_op jit(solution)/shard_map/ppermute | solution.py:12
  49.0 7.4 %pad_maximum_fusion = bf16[480,8192]{1,0:T(8,128)(2,1)} fusion(bf16[240,8192]{1,0:T(8,128)(2,1)} %param.8, bf16[240,8192]{1,0:T(8,128)(2,1)} %collective-permute-done), kind=kLoop, calls=%fused_computation.11 | loop fusion | flops 15728640 | bytes 15728640 | tf_op jit(solution)/shard_map/concatenate | solution.py:43
  56.4 12.8 %reshape.12 = bf16[30720,128]{1,0:T(8,128)(2,1)} reshape(bf16[480,8192]{1,0:T(8,128)(2,1)} %pad_maximum_fusion) | data formatting | bytes 15728640 | tf_op jit(solution)/shard_map/reshape | solution.py:43
  69.2 59.7 %gather_fusion = bf16[16384,128]{1,0:T(8,128)(2,1)} fusion(bf16[30720,128]{1,0:T(8,128)(2,1)} %reshape.12, s32[16384]{0:T(1024)S(1)} %broadcast_clamp_fusion), kind=kCustom, calls=%fused_computation | custom fusion | bytes 8454144 | tf_op jit(solution)/shard_map/gather | solution.py:45
  128.9 0.0 copy-start
  128.9 0.0 copy-start.1
  128.9 6.0 %fusion.5 = f32[1024]{0:T(1024)S(1)} fusion(bf16[1024,128,16]{1,2,0:T(8,128)(2,1)} %bitcast.6, bf16[1024,16,128]{2,1,0:T(8,128)(2,1)} %param.10), kind=kLoop, calls=%fused_computation.9 | loop fusion | flops 8387584 | bytes 8392704 | tf_op jit(solution)/shard_map/onc,onc->o/dot_general | solution.py:46
  134.9 16.3 %psum.7 = f32[1024]{0:T(1024)S(1)} all-reduce(f32[1024]{0:T(1024)S(1)} %fusion.5), channel_id=1, replica_groups=mesh['win'=16,'tile'=8] {'tile'}, use_global_device_ids=true, to_apply=%region_0.0 | all-reduce | flops 1024 | bytes 8192 | tf_op jit(solution)/shard_map/psum | solution.py:33
  151.2 0.0 copy-done
  151.2 0.0 copy-done.1
  151.2 6.4 %convert_multiply_fusion.1 = f32[1024,16,128]{2,1,0:T(8,128)} fusion(bf16[1024,16,128]{2,1,0:T(8,128)(2,1)} %param.10, f32[1024]{0:T(1024)S(1)} %subtract_multiply_fusion), kind=kLoop, calls=%fused_computation.10 | loop fusion | flops 4194304 | bytes 12587008 | tf_op jit(solution)/shard_map/mul | solution.py:48
  157.7 94.1 %scatter_custom_fusion = f32[30720,128]{1,0:T(8,128)} fusion(s32[16384]{0:T(1024)S(1)} %reshape.24, f32[16384,128]{1,0:T(8,128)} %bitcast.7, f32[]{:T(128)} %constant.5.clone.1), kind=kCustom, calls=%fused_computation.13 | custom fusion | flops 2097152 | bytes 15729152 | tf_op jit(solution)/shard_map/scatter-add | solution.py:49
  251.8 11.0 %fusion.23 = (f32[15360,128]{1,0:T(8,128)}, f32[15360,128]{1,0:T(8,128)}) fusion(f32[30720,128]{1,0:T(8,128)} %scatter_custom_fusion), kind=kLoop, calls=%fused_computation.35 | loop fusion | bytes 31457280 | tf_op jit(solution)/shard_map/slice | solution.py:53
  262.8 9.2 %slice.21 = f32[240,8192]{1,0:T(8,128)} reshape(f32[15360,128]{1,0:T(8,128)} %get-tuple-element.7) | data formatting | bytes 15728640 | tf_op jit(solution)/shard_map/slice | solution.py:53
  272.0 2.1 collective-permute-start.1
  274.1 9.2 %slice.19 = f32[240,8192]{1,0:T(8,128)} reshape(f32[15360,128]{1,0:T(8,128)} %get-tuple-element.8) | data formatting | bytes 15728640 | tf_op jit(solution)/shard_map/slice | solution.py:54
  283.3 84.7 %collective-permute-done.1 = f32[240,8192]{1,0:T(8,128)} collective-permute-done((f32[240,8192]{1,0:T(8,128)}, f32[240,8192]{1,0:T(8,128)}, u32[]{:S(2)}, u32[]{:S(2)}) %collective-permute-start.1) | collective-permute-done | bytes 7864352 | tf_op jit(solution)/shard_map/ppermute | solution.py:12
  368.1 13.1 %add_multiply_fusion = f32[240,8192]{1,0:T(8,128)} fusion(f32[240,8192]{1,0:T(8,128)} %param.9, f32[240,8192]{1,0:T(8,128)} %slice.19, f32[240,8192]{1,0:T(8,128)} %collective-permute-done.1), kind=kLoop, calls=%fused_computation.12 | loop fusion | flops 3932160 | bytes 31457280 | tf_op jit(solution)/shard_map/mul | solution.py:55
  381.2 1.5 fusion.24
  382.6 1.9 collective-permute-start.2
  384.6 2.5 collective-permute-start.3
  387.0 6.5 %collective-permute-done.2 = f32[24,8192]{1,0:T(8,128)S(1)} collective-permute-done((f32[24,8192]{1,0:T(8,128)S(1)}, f32[24,8192]{1,0:T(8,128)S(1)}, u32[]{:S(2)}, u32[]{:S(2)}) %collective-permute-start.2) | collective-permute-done | bytes 786464 | tf_op jit(solution)/shard_map/ppermute | solution.py:23
  393.5 11.3 %collective-permute-done.3 = f32[24,8192]{1,0:T(8,128)S(1)} collective-permute-done((f32[24,8192]{1,0:T(8,128)S(1)}, f32[24,8192]{1,0:T(8,128)S(1)}, u32[]{:S(2)}, u32[]{:S(2)}) %collective-permute-start.3) | collective-permute-done | bytes 786464 | tf_op jit(solution)/shard_map/ppermute | solution.py:25
  404.8 17.5 %convolution_multiply_fusion = f32[240,8192]{1,0:T(8,128)} fusion(f32[240,8192]{1,0:T(8,128)} %param.9, f32[24,8192]{1,0:T(8,128)S(1)} %collective-permute-done.3, f32[240,8192]{1,0:T(8,128)} %add_multiply_fusion, f32[24,8192]{1,0:T(8,128)S(1)} %collective-permute-done.2), kind=kOutput, calls=%fused_computation.2 | convolution fusion | flops 6801940992 | bytes 25165824 | tf_op jit(solution)/shard_map/dot_general | solution.py:63
  (2 shorter events, 0.0 us)
Async XLA Ops:
  0.0 49.0 %collective-permute-start = (bf16[240,8192]{1,0:T(8,128)(2,1)}, bf16[240,8192]{1,0:T(8,128)(2,1)}, u32[]{:S(2)}, u32[]{:S(2)}) collective-permute-start(bf16[240,8192]{1,0:T(8,128)(2,1)} %param.8), channel_id=1, source_target_pairs={{0,8},{8,16},{16,24},{24,32},{32,40},{40,48},{48,56},{56,64},{64,7... | collective-permute-start | bytes 11796488 | tf_op jit(solution)/shard_map/ppermute | solution.py:12
  128.9 22.3 %copy-start = (f32[1024]{0:T(1024)S(1)}, f32[1024]{0:T(1024)}, u32[]{:S(2)}) copy-start(f32[1024]{0:T(1024)} %param.12) | copy-start | bytes 12292
  128.9 22.3 %copy-start.1 = (f32[1024]{0:T(1024)S(1)}, f32[1024]{0:T(1024)}, u32[]{:S(2)}) copy-start(f32[1024]{0:T(1024)} %param.11) | copy-start | bytes 12292
  272.0 96.1 %collective-permute-start.1 = (f32[240,8192]{1,0:T(8,128)}, f32[240,8192]{1,0:T(8,128)}, u32[]{:S(2)}, u32[]{:S(2)}) collective-permute-start(f32[240,8192]{1,0:T(8,128)} %slice.21), channel_id=1, source_target_pairs={{8,0},{16,8},{24,16},{32,24},{40,32},{48,40},{56,48},{64,56},{72,6... | collective-permute-start | bytes 23592968 | tf_op jit(solution)/shard_map/ppermute | solution.py:12
  382.6 10.8 %collective-permute-start.2 = (f32[24,8192]{1,0:T(8,128)S(1)}, f32[24,8192]{1,0:T(8,128)S(1)}, u32[]{:S(2)}, u32[]{:S(2)}) collective-permute-start(f32[24,8192]{1,0:T(8,128)S(1)} %get-tuple-element.9), channel_id=1, source_target_pairs={{0,8},{8,16},{16,24},{24,32},{32,40},{40,48},{48,56},{56,64},{64,7... | collective-permute-start | bytes 2359304 | tf_op jit(solution)/shard_map/ppermute | solution.py:23
  384.6 20.2 %collective-permute-start.3 = (f32[24,8192]{1,0:T(8,128)S(1)}, f32[24,8192]{1,0:T(8,128)S(1)}, u32[]{:S(2)}, u32[]{:S(2)}) collective-permute-start(f32[24,8192]{1,0:T(8,128)S(1)} %get-tuple-element.10), channel_id=1, source_target_pairs={{8,0},{16,8},{24,16},{32,24},{40,32},{48,40},{56,48},{64,56},{72,6... | collective-permute-start | bytes 2359304 | tf_op jit(solution)/shard_map/ppermute | solution.py:25
where the time goes:
time: 423 us; the launch traced here: 422 us
  waiting for transfers between devices  143 us (34%)
  other arithmetic  129 us (30%)
  local copies, waits for them, and re-layouts  104 us (25%)
  matrix products  17.5 us (4%)
  blocking collectives  16.3 us (4%)
  starting transfers between devices  12.5 us (3%)
    ppermute x2, waiting for transfers between devices, from_behind(): lax.ppermute(value, axis, [(source, source + steps) for source in range(i...  125 us
    scatter-add x1, other arithmetic, shards(): jax.ops.segment_sum(contrib.reshape(-1, width), flat.reshape(-1), num_seg...  94.1 us
    gather x1, local copies, waits for them, and re-layouts, shards(): picked = joined[flat]  59.7 us
    slice x2, local copies, waits for them, and re-layouts, shards(): returned = from_behind(summed[:hours], 'win', -1)  20.3 us
    dot_general x1, matrix products, shards(): jnp.dot(kernel, rim, preferred_element_type=jnp.float32, precision=lax.Pr...  17.5 us
    psum x1, blocking collectives, misfits(): predicted = lax.psum(partial_value, 'tile')  16.3 us
    mul x1, other arithmetic, shards(): scaled = prior_std * adjoint  13.1 us
    reshape x1, local copies, waits for them, and re-layouts, shards(): jnp.concatenate([earlier, flux], axis=0)  12.8 us
  transfers between devices with their start and end apart: 4, of which 4 were waited for; matrix products, arithmetic and copies ran while one was open for 3% of the time, Pallas kernels for 0%

commit v1 on v0

--- a/solution.py
+++ b/solution.py
@@ -1,9 +1,44 @@
+import functools
+
 import jax
 import jax.numpy as jnp
+import numpy as np
 from jax import lax
+from jax.experimental import pallas as pl
+from jax.experimental.pallas import tpu as pltpu
 from jax.sharding import PartitionSpec as P
 
 KH = 24
+LANES = 128
+CELLS = 64
+NBIN = 2 * CELLS
+HEAD = 41 * LANES
+NEAR = 32
+META = CELLS + CELLS + 8
+F32, BF16, I32 = jnp.float32, jnp.bfloat16, jnp.int32
+NT = (((1,), (1,)), ((), ()))
+MESH = pl.DeviceIdType.MESH
+VM = pl.BlockSpec(memory_space=pltpu.VMEM)
+ANY = pl.BlockSpec(memory_space=pl.ANY)
+TAB = pl.BlockSpec((8, LANES), lambda *_: (META // 8 - 1, 0), memory_space=pltpu.SMEM)
+TABV = pl.BlockSpec((8, LANES), lambda *_: (META // 8 - 1, 0))
+
+
+def iota(shape, dim):
+    return lax.broadcasted_iota(I32, shape, dim)
+
+
+def dot(a, b):
+    return jnp.dot(a, b, preferred_element_type=F32)
+
+
+def halves(v):
+    top = v.astype(BF16).astype(F32)
+    return top, v - top
+
+
+def pick(table, lane):
+    return jnp.take_along_axis(table, jnp.broadcast_to(lane, table.shape), axis=1, mode="promise_in_bounds")
 
 
 def from_behind(value, axis, steps):
@@ -34,7 +69,7 @@
     return (predicted - obs_value) * obs_weight
 
 
-def shards(flux, prior_std, footprint, obs_value, obs_weight, obs_hour, hour_offset, block_cell):
+def general(flux, prior_std, footprint, obs_value, obs_weight, obs_hour, hour_offset, block_cell):
     hours = flux.shape[0]
     cells = flux.shape[1]
     width = footprint.shape[2]
@@ -66,6 +101,670 @@
     return prior_std * smoothed
 
 
+def sort_body(nobs, which, hb, oh_ref, off_ref, cell_ref, fp_ref, own_ref, neg_ref, ometa_ref, nmeta_ref,
+              fpv, stage, rows, outv, keyv, hourv, posv, poss, metav, tabs, tabv, sems):
+    nblk = off_ref.shape[0]
+    n = nobs * nblk
+    per = nobs // LANES
+    lines = nblk * per
+    cap = n + CELLS * 16 + LANES
+    span = HEAD // LANES - 1
+    fetch = pltpu.make_async_copy(fp_ref.at[pl.ds(which * n, n)], fpv, sems.at[0])
+    fetch.start()
+    bins = iota((NBIN, LANES), 0)
+    lanes = iota((NBIN, LANES), 1)
+    upper = (bins < lanes).astype(BF16)
+    ones = jnp.ones((LANES, LANES), BF16)
+    same = (bins // CELLS) == (lanes // CELLS)
+    below = jnp.where(same & (lanes < bins), 1.0, 0.0).astype(BF16)
+    before = jnp.where(same & (bins < lanes), 1.0, 0.0).astype(BF16)
+
+    for c in range(per):
+        cut = slice(which * nobs + c * LANES, which * nobs + (c + 1) * LANES)
+        hour = oh_ref[:, cut] - off_ref[:, cut]
+        early = hour < 0
+        hour = jnp.where(early, hour + hb, hour)
+        key = jnp.where(early, cell_ref[:, cut] + CELLS, cell_ref[:, cut])
+        rim = (hour < KH) | (hour >= hb - KH)
+        at = slice(c * nblk, (c + 1) * nblk)
+        keyv[0, at, :] = jnp.where(rim, key, -1)
+        keyv[1, at, :] = jnp.where(rim, -1, key)
+        keyv[2, at, :] = key
+        hourv[at, :] = (hour + 1).astype(F32)
+
+    def count(r, total):
+        first, second = total
+        for u in range(4):
+            first = first + jnp.where(bins == keyv[0, pl.ds(r * 4 + u, 1), :], 1.0, 0.0)
+            second = second + jnp.where(bins == keyv[1, pl.ds(r * 4 + u, 1), :], 1.0, 0.0)
+        return first, second
+
+    zero = jnp.zeros((NBIN, LANES), F32)
+    first, second = lax.fori_loop(0, lines // 4, count, (zero, zero))
+    first, second = first.astype(BF16), second.astype(BF16)
+    ahead = [dot(v, upper) for v in (first, second)]
+    rim_s = dot(first, ones)
+    cnt_s = rim_s + dot(second, ones)
+    rim_l = lax.dot_general(ones[:8], first, NT, preferred_element_type=F32)
+    cnt_l = rim_l + lax.dot_general(ones[:8], second, NT, preferred_element_type=F32)
+
+    def starts(cnt, left):
+        tiles = jnp.floor((cnt + 15.0) * (1.0 / 16.0))
+        coarse = jnp.floor(tiles * (1.0 / 128.0))
+        fine = tiles - 128.0 * coarse
+
+        def run(v):
+            return dot(below, v.astype(BF16)) if left else dot(v.astype(BF16), before)
+
+        return 16.0 * (128.0 * run(coarse) + run(fine))
+
+    tight_l = starts(cnt_l, False)
+    base = starts(cnt_s, True) + jnp.where(bins >= CELLS, float(cap), 0.0)
+    line8 = iota((8, LANES), 0)
+    limit = float(span * LANES)
+    far = jnp.where((cnt_l > float(LANES)) | (rim_l > float(NEAR)) | (tight_l + cnt_l > limit), 1.0, 0.0)
+    over = jnp.max(far, axis=1, keepdims=True)
+    tab = jnp.where(line8 == 0, jnp.minimum(cnt_l, float(LANES)),
+                    jnp.where(line8 == 1, jnp.minimum(tight_l, limit), over)).astype(I32)
+    tabv[...] = tab
+    metav[0, 2 * CELLS:META, :] = tab
+    metav[1, 2 * CELLS:META, :] = pltpu.roll(tab, CELLS, 1)
+    to_tab = pltpu.make_async_copy(tabv, tabs, sems.at[1])
+    to_tab.start()
+
+    for turn in range(2):
+        def place(r, acc):
+            for u in range(4):
+                at = pl.ds(r * 4 + u, 1)
+                hot = bins == keyv[turn, at, :]
+                posf = jnp.sum(jnp.where(hot, acc, 0.0), axis=0, keepdims=True).astype(I32)
+                posv[at, :] = posf if turn == 0 else posv[at, :] + posf
+                acc = jnp.where(hot, acc + 1.0, acc)
+            return acc
+
+        lax.fori_loop(0, lines // 4, place, base + ahead[turn] + (rim_s if turn else 0.0))
+    to_pos = pltpu.make_async_copy(posv, poss, sems.at[2])
+    to_pos.start()
+    starts_l = tight_l + jnp.where(iota((8, LANES), 1) >= CELLS, float(cap), 0.0)
+    for g in range(lines // 8):
+        at = slice(g * 8, (g + 1) * 8)
+        key = keyv[2, at, :]
+        rank = posv[at, :] - pick(starts_l, key).astype(I32)
+        keyv[0, at, :] = rank
+        spot = jnp.where(rank < LANES, (key & (CELLS - 1)) * LANES + rank, -1)
+        metav[0, CELLS + g * 8:CELLS + (g + 1) * 8, :] = jnp.where(key < CELLS, spot, -1)
+        metav[1, CELLS + g * 8:CELLS + (g + 1) * 8, :] = jnp.where(key < CELLS, -1, spot)
+
+    obs = iota((1, LANES), 1).astype(F32)
+    done = zero
+    for c in range(per):
+        def gather(r, acc):
+            marks, spots = [], []
+            for u in range(4):
+                at = pl.ds(c * nblk + r * 4 + u, 1)
+                hot = bins == keyv[2, at, :]
+                marks.append(jnp.concatenate(
+                    [jnp.where(hot, v, 0.0).astype(BF16) for v in (hourv[at, :], obs)], axis=0))
+                spots.append(jnp.where(bins == keyv[0, at, :], 1.0, 0.0).astype(BF16))
+            return acc + lax.dot_general(jnp.concatenate(marks, axis=1), jnp.concatenate(spots, axis=1), NT,
+                                         preferred_element_type=F32)
+
+        acc = lax.fori_loop(0, nblk // 4, gather, jnp.zeros((2 * NBIN, LANES), F32))
+        hour, low = acc[:NBIN], acc[NBIN:]
+        done = done + jnp.where(hour > 0.0, hour + 256.0 * (low + float(c * LANES)), 0.0)
+    done = done.astype(I32)
+    metav[0, 0:CELLS, :] = done[:CELLS]
+    metav[1, 0:CELLS, :] = done[CELLS:]
+    to_meta = [pltpu.make_async_copy(metav.at[k], ref, sems.at[3 + k]) for k, ref in enumerate((ometa_ref, nmeta_ref))]
+    for copy in to_meta:
+        copy.start()
+    to_tab.wait()
+    blocks = []
+    for side in range(2):
+        last = CELLS - 1 + CELLS * side
+        end = jnp.minimum(tabs[1, last] + tabs[0, last], span * LANES)
+        blocks.append(jnp.minimum(lax.shift_right_logical(end + 270, 7), span + 1))
+
+    for side in range(2):
+        def blank(i, _):
+            at = pl.multiple_of(i * LANES + side * cap, LANES)
+            rows[pl.ds(at, LANES), :] = jnp.zeros((LANES, LANES), F32)
+            return 0
+
+        lax.fori_loop(0, blocks[side], blank, 0)
+    fetch.wait()
+
+    def unpack(i, _):
+        for u in range(8):
+            at = pl.multiple_of(i * 128 + u * 16, 16)
+            stage[pl.ds(at, 16), :] = fpv[pl.ds(at, 16), :].astype(F32)
+        return 0
+
+    lax.fori_loop(0, n // 128, unpack, 0)
+    to_pos.wait()
+
+    def permute(r, _):
+        c = lax.shift_right_logical(r, 4)
+        src = c * (LANES * nblk) + (r & 15)
+        for l in range(LANES):
+            rows[pl.ds(poss[r, l], 1), :] = stage[pl.ds(src + l * nblk, 1), :]
+        return 0
+
+    lax.fori_loop(0, lines, permute, 0)
+    copies = []
+    for side in (1, 0):
+        def convert(i, _):
+            at = pl.multiple_of(i * 128, 128)
+            src = pl.multiple_of(at + side * cap, 128)
+            outv[side, pl.ds(at, 128), :] = rows[pl.ds(src, 128), :].astype(BF16)
+            return 0
+
+        lax.fori_loop(0, blocks[side], convert, 0)
+        copies.append(pltpu.make_async_copy(outv.at[side], (own_ref, neg_ref)[side], sems.at[5 + side]))
+        copies[-1].start()
+    for copy in to_meta + copies:
+        copy.wait()
+
+
+def sort_half(oh, off, cell, fp2, which, hb):
+    nblk, count = off.shape
+    nobs = count // 2
+    n = nobs * nblk
+    cap = n + CELLS * 16 + LANES
+    lines = nblk * nobs // LANES
+    return pl.pallas_call(
+        functools.partial(sort_body, nobs, which, hb),
+        out_shape=(jax.ShapeDtypeStruct((HEAD, LANES), BF16), jax.ShapeDtypeStruct((HEAD, LANES), BF16),
+                   jax.ShapeDtypeStruct((META, LANES), I32), jax.ShapeDtypeStruct((META, LANES), I32)),
+        in_specs=[VM, VM, VM, ANY],
+        out_specs=(ANY, ANY, ANY, ANY),
+        scratch_shapes=[
+            pltpu.VMEM((n, LANES), BF16), pltpu.VMEM((n, LANES), F32), pltpu.VMEM((2 * cap, LANES), F32),
+            pltpu.VMEM((2, HEAD, LANES), BF16), pltpu.VMEM((3, lines, LANES), I32), pltpu.VMEM((lines, LANES), F32),
+            pltpu.VMEM((lines, LANES), I32), pltpu.SMEM((lines, LANES), I32),
+            pltpu.VMEM((2, META, LANES), I32), pltpu.SMEM((8, LANES), I32),
+            pltpu.VMEM((8, LANES), I32), pltpu.SemaphoreType.DMA((7,)),
+        ],
+        compiler_params=pltpu.CompilerParams(vmem_limit_bytes=40 << 20),
+        cost_estimate=pl.CostEstimate(flops=10**9, bytes_accessed=50 << 20, transcendentals=0),
+        name="sort_half",
+    )(oh, off, cell, fp2)
+
+
+def predict_body(k, slot, chained, *refs):
+    flux_ref, rows, metas, tabs = refs[0], refs[1:1 + k], refs[1 + k:1 + 2 * k], refs[1 + 2 * k:1 + 3 * k]
+    before_ref = refs[1 + 3 * k] if chained else None
+    out_ref, fluxv, rowv, tablev, sems = refs[-5:]
+    cells = flux_ref.shape[1]
+    parts = 4
+    wide = cells // parts
+    loads = [pltpu.make_async_copy(rows[i], rowv.at[i], sems.at[i]) for i in range(k)]
+    flows = [pltpu.make_async_copy(flux_ref.at[:, pl.ds(p * wide, wide)], fluxv.at[:, pl.ds(p * wide, wide)],
+                                   sems.at[k + p]) for p in range(parts)]
+    flows[0].start()
+    for load in loads:
+        load.start()
+    for flow in flows[1:]:
+        flow.start()
+    hours = iota((flux_ref.shape[0], k * LANES), 0) + 1
+    for load in loads:
+        load.wait()
+    for p in range(parts):
+        flows[p].wait()
+
+        def group(g, _):
+            for u in range(4):
+                b = p * (CELLS // parts) + g * 4 + u
+                hour = jnp.concatenate([m[pl.ds(b, 1), :] & 255 for m in metas], axis=1)
+                fp = jnp.concatenate(
+                    [rowv[i, pl.ds(pl.multiple_of(tabs[i][1, b], 16), LANES), :] for i in range(k)], axis=0)
+                local = fluxv[:, pl.ds(pl.multiple_of(b * LANES, LANES), LANES)]
+                full = lax.dot_general(local, fp, NT, preferred_element_type=F32)
+                value = jnp.sum(jnp.where(hours == hour, full, 0.0), axis=0, keepdims=True)
+                for i in range(k):
+                    tablev[i, pl.ds(b, 1), :] = value[:, i * LANES:(i + 1) * LANES]
+            return 0
+
+        lax.fori_loop(0, CELLS // parts // 4, group, 0)
+    per = 4
+    lines = []
+    for i in range(k):
+        spots = [metas[i][CELLS + g * 8:CELLS + (g + 1) * 8, :] for g in range(8)]
+        cell = [lax.shift_right_arithmetic(s, 7) for s in spots]
+        lane = [s & 127 for s in spots]
+
+        def collect(b, acc):
+            row = jnp.broadcast_to(tablev[i, pl.ds(b, 1), :], (8, LANES))
+            acc = list(acc)
+            for g in range(8):
+                acc[g // 2] = acc[g // 2] + jnp.where(cell[g] == b, pick(row, lane[g]), 0.0)
+            return tuple(acc)
+
+        acc = lax.fori_loop(0, CELLS, collect, (jnp.zeros((8, LANES), F32),) * per)
+        lines.append(jnp.concatenate([jnp.sum(a, axis=0, keepdims=True) for a in acc], axis=0))
+    if k == 2:
+        out_ref[...] = jnp.concatenate(lines, axis=0)
+    else:
+        blank = jnp.zeros((per, LANES), F32)
+        both = jnp.concatenate([lines[0], blank] if slot == 0 else [blank, lines[0]], axis=0)
+        out_ref[...] = both + before_ref[...] if chained else both
+
+
+def predict(flux, pairs, slot=0, before=None):
+    k = len(pairs)
+    rows, metas = [r for r, _ in pairs], [m for _, m in pairs]
+    more = [] if before is None else [before]
+    return pl.pallas_call(
+        functools.partial(predict_body, k, slot, before is not None),
+        grid=(1,),
+        out_shape=jax.ShapeDtypeStruct((8, LANES), F32),
+        in_specs=[ANY] + [ANY] * k + [VM] * k + [TAB] * k + [VM] * len(more),
+        out_specs=VM,
+        scratch_shapes=[pltpu.VMEM(flux.shape, BF16), pltpu.VMEM((k, HEAD, LANES), BF16),
+                        pltpu.VMEM((k, CELLS, LANES), F32), pltpu.SemaphoreType.DMA((k + 4,))],
+        compiler_params=pltpu.CompilerParams(vmem_limit_bytes=20 << 20),
+        cost_estimate=pl.CostEstimate(flops=k * 2 * 240 * 8192 * 128, bytes_accessed=(10 + 5 * k) << 20,
+                                      transcendentals=0),
+        name="predict",
+    )(flux, *rows, *metas, *metas, *more)
+
+
+def exchange_body(own_ref, next_ref, obs_ref, tab0_ref, tab1_ref, w_ref, bad_ref,
+                  pair_o, pair_n, prev_n, next_o, next_obs, flags, mine, spread_bad,
+                  s_pair, s_side, s_flag, r_pair, r_side, r_obs, r_flag, s_bad, r_bad):
+    wins, tiles = lax.axis_size("win"), lax.axis_size("tile")
+    w, t = lax.axis_index("win"), lax.axis_index("tile")
+    up, down = w > 0, w < wins - 1
+    barrier = pltpu.get_barrier_semaphore()
+
+    def greet(device):
+        pl.semaphore_signal(barrier, inc=1, device_id=device, device_id_type=MESH)
+
+    peers = [lax.rem(t + d, tiles) for d in range(tiles)]
+    others = [lax.rem(w + d, wins) for d in range(wins)]
+    for d in range(1, tiles):
+        greet((w, peers[d]))
+    for d in range(1, wins):
+        greet((others[d], t))
+
+    @pl.when(up)
+    def _():
+        for d in range(1, tiles):
+            greet((w - 1, peers[d]))
+
+    @pl.when(down)
+    def _():
+        for d in range(1, tiles):
+            greet((w + 1, peers[d]))
+
+    sides = jnp.where(up, 1, 0) + jnp.where(down, 1, 0)
+    pl.semaphore_wait(barrier, tiles - 1 + wins - 1 + sides * (tiles - 1))
+
+    def push(src, dst, ssem, rsem, device):
+        return pltpu.make_async_remote_copy(src_ref=src, dst_ref=dst, send_sem=ssem, recv_sem=rsem,
+                                            device_id=device, device_id_type=MESH)
+
+    def to_peer(d):
+        return [push(own_ref, pair_o.at[t], s_pair.at[0, d], r_pair.at[0, t], (w, peers[d])),
+                push(next_ref, pair_n.at[t], s_pair.at[1, d], r_pair.at[1, t], (w, peers[d]))]
+
+    def to_up(d):
+        return push(own_ref, next_o.at[t], s_side.at[0, d], r_side.at[0, t], (w - 1, peers[d]))
+
+    def to_down(d):
+        return push(next_ref, prev_n.at[t], s_side.at[1, d], r_side.at[1, t], (w + 1, peers[d]))
+
+    def obs_up():
+        return push(obs_ref, next_obs, s_side.at[2, 0], r_obs, (w - 1, t))
+
+    def to_flag(d):
+        return [push(tab0_ref, flags.at[0, w], s_flag.at[0, d], r_flag.at[0, w], (others[d], t)),
+                push(tab1_ref, flags.at[1, w], s_flag.at[1, d], r_flag.at[1, w], (others[d], t))]
+
+    def from_peer(d):
+        q = peers[d]
+        return [push(own_ref, pair_o.at[q], s_pair.at[0, d], r_pair.at[0, q], (w, q)),
+                push(next_ref, pair_n.at[q], s_pair.at[1, d], r_pair.at[1, q], (w, q))]
+
+    def from_down(d):
+        q = peers[d]
+        return push(own_ref, next_o.at[q], s_side.at[0, d], r_side.at[0, q], (w - 1, q))
+
+    def from_up(d):
+        q = peers[d]
+        return push(next_ref, prev_n.at[q], s_side.at[1, d], r_side.at[1, q], (w + 1, q))
+
+    def from_flag(d):
+        v = others[d]
+        return [push(tab0_ref, flags.at[0, v], s_flag.at[0, d], r_flag.at[0, v], (v, t)),
+                push(tab1_ref, flags.at[1, v], s_flag.at[1, d], r_flag.at[1, v], (v, t))]
+
+    for d in range(1, wins):
+        for copy in to_flag(d):
+            copy.start()
+
+    @pl.when(up)
+    def _():
+        obs_up().start()
+        for d in range(tiles):
+            to_up(d).start()
+
+    @pl.when(down)
+    def _():
+        for d in range(tiles):
+            to_down(d).start()
+
+    for d in range(1, tiles):
+        for copy in to_peer(d):
+            copy.start()
+
+    bad = jnp.maximum(tab0_ref[...], tab1_ref[...])
+    for d in range(1, wins):
+        for k, copy in enumerate(from_flag(d)):
+            copy.wait_recv()
+            bad = jnp.maximum(bad, flags[k, others[d]])
+    mine[...] = bad
+    own, later = own_ref[...], next_ref[...]
+    for d in range(1, tiles):
+        for copy in from_peer(d):
+            copy.wait_recv()
+        own = own + pair_o[peers[d]]
+        later = later + pair_n[peers[d]]
+    for d in range(1, tiles):
+        push(mine, spread_bad.at[t], s_bad.at[d], r_bad.at[t], (w, peers[d])).start()
+    w_ref[0] = own
+    w_ref[1] = later
+
+    @pl.when(up)
+    def _():
+        total = w_ref[0]
+        for d in range(tiles):
+            from_up(d).wait_recv()
+            total = total + prev_n[peers[d]]
+        w_ref[0] = total
+
+    w_ref[0] = (w_ref[0] - obs_ref[0]) * obs_ref[1]
+
+    @pl.when(down)
+    def _():
+        total = w_ref[1]
+        for d in range(tiles):
+            from_down(d).wait_recv()
+            total = total + next_o[peers[d]]
+        pltpu.make_async_remote_copy(src_ref=obs_ref, dst_ref=next_obs, send_sem=s_side.at[2, 0], recv_sem=r_obs,
+                                     device_id=(w + 1, t), device_id_type=MESH).wait_recv()
+        w_ref[1] = (total - next_obs[0]) * next_obs[1]
+
+    for d in range(1, tiles):
+        q = peers[d]
+        push(mine, spread_bad.at[q], s_bad.at[d], r_bad.at[q], (w, q)).wait_recv()
+        bad = jnp.maximum(bad, spread_bad[q])
+    bad_ref[...] = bad
+    for d in range(1, wins):
+        for copy in to_flag(d):
+            copy.wait_send()
+    for d in range(1, tiles):
+        for copy in to_peer(d):
+            copy.wait_send()
+        push(mine, spread_bad.at[t], s_bad.at[d], r_bad.at[t], (w, peers[d])).wait_send()
+
+    @pl.when(up)
+    def _():
+        obs_up().wait_send()
+        for d in range(tiles):
+            to_up(d).wait_send()
+
+    @pl.when(down)
+    def _():
+        for d in range(tiles):
+            to_down(d).wait_send()
+
+
+def exchange(mine, other, obs, metas):
+    wins, tiles = lax.axis_size("win"), lax.axis_size("tile")
+    block = pltpu.VMEM((tiles, 8, LANES), F32)
+    sem = pltpu.SemaphoreType.DMA
+    return pl.pallas_call(
+        exchange_body,
+        grid=(1,),
+        out_shape=(jax.ShapeDtypeStruct((2, 8, LANES), F32), jax.ShapeDtypeStruct((8, LANES), I32)),
+        in_specs=[VM, VM, VM, TABV, TABV],
+        out_specs=(VM, VM),
+        scratch_shapes=[block, block, block, block, pltpu.VMEM((2, 8, LANES), F32),
+                        pltpu.VMEM((2, wins, 8, LANES), I32), pltpu.VMEM((8, LANES), I32),
+                        pltpu.VMEM((tiles, 8, LANES), I32),
+                        sem((2, tiles)), sem((3, tiles)), sem((2, wins)), sem((2, tiles)), sem((2, tiles)), sem,
+                        sem((2, wins)), sem((tiles,)), sem((tiles,))],
+        compiler_params=pltpu.CompilerParams(collective_id=3, has_side_effects=True),
+        name="exchange",
+    )(mine, other, obs, *metas)
+
+
+def weigh(code, tables, slots):
+    got = [pick(table, lax.shift_right_logical(code, 8) & 127) for table in tables]
+    got = got[0] if len(got) == 1 else jnp.where(iota((8, LANES), 1) < 2 * NEAR, got[0], got[1])
+    mine = iota((8, LANES), 0) == lax.shift_right_logical(code, 15) + slots
+    return jnp.sum(jnp.where(mine, got, 0.0), axis=0, keepdims=True)
+
+
+def spread(hour, hours, w):
+    hit = hours == hour
+    return [jnp.where(hit, v, 0.0).astype(BF16) for v in halves(w)]
+
+
+def edges_body(w_ref, ps_head, ps_tail, *refs):
+    rows, metas, tabs = refs[0:4], refs[4:8], refs[8:12]
+    head_ref, tail_ref, rowv, sems = refs[12:]
+    loads = [pltpu.make_async_copy(rows[i], rowv.at[i], sems.at[i]) for i in range(4)]
+    for load in loads:
+        load.start()
+    total = 240
+    band = iota((2 * KH, LANES), 0)
+    hours = jnp.where(band < KH, band, band + (total - 2 * KH)) + 1
+    quarter = lax.shift_right_logical(iota((1, LANES), 1), 5)
+    slots = (quarter & 1) * 4
+    tables = [w_ref[0], w_ref[1]]
+    for load in loads:
+        load.wait()
+
+    def group(g, _):
+        for u in range(4):
+            b = g * 4 + u
+            code = metas[0][pl.ds(b, 1), :]
+            fps = []
+            for i in range(4):
+                if i:
+                    code = jnp.where(quarter == i, pltpu.roll(metas[i][pl.ds(b, 1), :], i * NEAR, 1), code)
+                fps.append(rowv[i, pl.ds(pl.multiple_of(tabs[i][1, b], 16), NEAR), :])
+            fp = jnp.concatenate(fps, axis=0)
+            left = jnp.concatenate(spread(code & 255, hours, weigh(code, tables, slots)), axis=1)
+            part = dot(left, jnp.concatenate([fp, fp], axis=0))
+            col = pl.ds(pl.multiple_of(b * LANES, LANES), LANES)
+            head_ref[:, col] = part[:KH] * ps_head[:, col]
+            tail_ref[:, col] = part[KH:] * ps_tail[:, col]
+        return 0
+
+    lax.fori_loop(0, CELLS // 4, group, 0)
+
+
+def edges(w, ps, pairs):
+    rows, metas = [r for r, _ in pairs], [m for _, m in pairs]
+    cells = ps.shape[1]
+    last = ps.shape[0] // KH - 1
+    return pl.pallas_call(
+        edges_body,
+        grid=(1,),
+        out_shape=(jax.ShapeDtypeStruct((KH, cells), F32), jax.ShapeDtypeStruct((KH, cells), F32)),
+        in_specs=[VM, pl.BlockSpec((KH, cells), lambda *_: (0, 0)), pl.BlockSpec((KH, cells), lambda *_: (last, 0))]
+        + [ANY] * 4 + [VM] * 4 + [TAB] * 4,
+        out_specs=(VM, VM),
+        scratch_shapes=[pltpu.VMEM((4, HEAD, LANES), BF16), pltpu.SemaphoreType.DMA((4,))],
+        compiler_params=pltpu.CompilerParams(vmem_limit_bytes=20 << 20),
+        cost_estimate=pl.CostEstimate(flops=10**8, bytes_accessed=8 << 20, transcendentals=0),
+        name="edges",
+    )(w, ps, ps, *rows, *metas, *metas)
+
+
+def inner_body(w_ref, head_ref, tail_ref, kern_ref, ps_ref, *refs):
+    rows, metas, tabs = refs[0:4], refs[4:8], refs[8:12]
+    out_ref, rowv, psv, outv, sv, sems, osems = refs[12:]
+    total, cells = ps_ref.shape
+    parts = 16
+    wide = cells // parts
+    per = CELLS // parts
+    inside = total - 2 * KH
+    loads = [pltpu.make_async_copy(rows[i], rowv.at[i], sems.at[i]) for i in range(4)]
+
+    def flow(p):
+        at = pl.ds(pl.multiple_of(p * wide, LANES), wide)
+        return pltpu.make_async_copy(ps_ref.at[:, at], psv.at[:, at], sems.at[4 + p])
+
+    def drain(p):
+        at = pl.ds(pl.multiple_of(p * wide, LANES), wide)
+        return pltpu.make_async_copy(outv.at[p & 1], out_ref.at[:, at], osems.at[p & 1])
+
+    flow(0).start()
+    for load in loads:
+        load.start()
+    for p in range(1, parts):
+        flow(p).start()
+    hours = iota((inside, LANES), 0) + KH + 1
+    pad = jnp.zeros((16, wide), BF16)
+    for load in loads:
+        load.wait()
+
+    def part_of(p, _):
+        flow(p).wait()
+        for u in range(per):
+            b = p * per + u
+            left, right = [], []
+            for i in range(4):
+                code = metas[i][pl.ds(b, 1), :]
+                left += spread(code & 255, hours, weigh(code, [w_ref[i // 2]], (i % 2) * 4))
+                fp = rowv[i, pl.ds(pl.multiple_of(tabs[i][1, b], 16), LANES), :]
+                right += [fp, fp]
+            part = dot(jnp.concatenate(left, axis=1), jnp.concatenate(right, axis=0))
+            col = pl.ds(pl.multiple_of(b * LANES, LANES), LANES)
+            here = slice(u * LANES, (u + 1) * LANES)
+            sv[:KH, here] = head_ref[:, col]
+            sv[KH:total - KH, here] = part * psv[KH:total - KH, col]
+            sv[total - KH:, here] = tail_ref[:, col]
+        top, low = halves(sv[...])
+        top, low = top.astype(BF16), low.astype(BF16)
+        stack = jnp.concatenate([top, pad, low, pad, top, pad], axis=0)
+        smooth = dot(kern_ref[...], stack)
+
+        @pl.when(p >= 2)
+        def _():
+            drain(p - 2).wait()
+
+        outv[p & 1] = smooth * psv[:, pl.ds(pl.multiple_of(p * wide, LANES), wide)]
+        drain(p).start()
+        return 0
+
+    lax.fori_loop(0, parts, part_of, 0)
+    for p in (parts - 2, parts - 1):
+        drain(p).wait()
+
+
+def inner(w, head, tail, kern, ps, pairs):
+    rows, metas = [r for r, _ in pairs], [m for _, m in pairs]
+    wide = ps.shape[1] // 16
+    return pl.pallas_call(
+        inner_body,
+        grid=(1,),
+        out_shape=jax.ShapeDtypeStruct(ps.shape, F32),
+        in_specs=[VM, VM, VM, VM, ANY] + [ANY] * 4 + [VM] * 4 + [TAB] * 4,
+        out_specs=ANY,
+        scratch_shapes=[pltpu.VMEM((4, HEAD, LANES), BF16), pltpu.VMEM(ps.shape, F32),
+                        pltpu.VMEM((2, ps.shape[0], wide), F32), pltpu.VMEM((ps.shape[0], wide), F32),
+                        pltpu.SemaphoreType.DMA((20,)), pltpu.SemaphoreType.DMA((2,))],
+        compiler_params=pltpu.CompilerParams(vmem_limit_bytes=32 << 20),
+        cost_estimate=pl.CostEstimate(flops=4 * 10**9, bytes_accessed=40 << 20, transcendentals=0),
+        name="inner",
+    )(w, head, tail, kern, ps, *rows, *metas, *metas)
+
+
+def finish_body(own_ref, ps_ref, above_ref, below_ref, out_ref):
+    row = iota((KH, LANES), 0).astype(F32)
+
+    def fill(ref, scale, after, forward):
+        for c in range(out_ref.shape[1] // LANES):
+            cut = slice(c * LANES, (c + 1) * LANES)
+            x = ref[:, cut] * scale
+            for s in (1, 2, 4, 8, 16):
+                gap = jnp.zeros((s, LANES), F32)
+                x = x + (jnp.concatenate([gap, x[:KH - s]], axis=0) if forward
+                         else jnp.concatenate([x[s:], gap], axis=0))
+            out_ref[:, cut] = own_ref[:, cut] + ps_ref[:, cut] * (x * after)
+
+    @pl.when(pl.program_id(0) == 0)
+    def _():
+        fill(above_ref, jnp.exp((row - KH) * (2.0 / KH)), jnp.exp(row * (-2.0 / KH)), False)
+
+    @pl.when(pl.program_id(0) == 1)
+    def _():
+        fill(below_ref, jnp.exp(row * (-2.0 / KH)), jnp.exp((row - KH) * (2.0 / KH)), True)
+
+
+def finish(partial, ps, above, below):
+    cells = ps.shape[1]
+    last = ps.shape[0] // KH - 1
+    wide = 2048
+    edge = pl.BlockSpec((KH, wide), lambda s, c: (s * last, c))
+    return pl.pallas_call(
+        finish_body,
+        grid=(2, cells // wide),
+        out_shape=jax.ShapeDtypeStruct(ps.shape, F32),
+        in_specs=[edge, edge, pl.BlockSpec((KH, wide), lambda s, c: (0, jnp.where(s == 0, c, cells // wide - 1))),
+                  pl.BlockSpec((KH, wide), lambda s, c: (0, jnp.where(s == 0, 0, c)))],
+        out_specs=edge,
+        input_output_aliases={0: 0},
+        name="finish",
+    )(partial, ps, above, below)
+
+
+def taps(distance):
+    far = np.abs(distance)
+    full = np.where(far <= KH, np.exp(np.float32(-2.0) * far.astype(np.float32) / np.float32(KH)), 0).astype(np.float32)
+    top = full.astype(BF16)
+    return top, (full - top.astype(np.float32)).astype(BF16)
+
+
+def smoother(total):
+    row, col = np.arange(total)[:, None], np.arange(256)[None, :]
+    top, low = taps(np.where(col < total, row - col, total))
+    return jnp.asarray(np.concatenate([top, top, low], axis=1))
+
+
+def quick(flux, prior_std, w, pairs):
+    head, tail = edges(w, prior_std, pairs)
+    above = from_behind(tail, "win", 1)
+    below = from_behind(head, "win", -1)
+    partial = inner(w, head, tail, smoother(flux.shape[0]), prior_std, pairs)
+    return finish(partial, prior_std, above, below)
+
+
+def shards(flux, prior_std, footprint, obs_value, obs_weight, obs_hour, hour_offset, block_cell):
+    count, nblk, width = footprint.shape
+    own, theirs = [], []
+    for k in range(2):
+        rows, early, meta, early_meta = sort_half(
+            obs_hour.reshape(1, count), hour_offset.T, block_cell.T,
+            footprint.reshape(count * nblk, width), k, flux.shape[0])
+        own.append((rows, meta))
+        theirs.append((from_behind(early, "win", -1), from_behind(early_meta, "win", -1)))
+    obs = jnp.stack([obs_value.reshape(8, LANES), obs_weight.reshape(8, LANES)])
+    mine = predict(flux, own)
+    other = predict(flux, theirs[:1])
+    other = predict(flux, theirs[1:], 1, other)
+    w, bad = exchange(mine, other, obs, [meta for _, meta in own])
+    return lax.cond(
+        bad[2, 0] > 0,
+        lambda: general(flux, prior_std, footprint, obs_value, obs_weight, obs_hour, hour_offset, block_cell),
+        lambda: quick(flux, prior_std, w, own + theirs))
+
+
 def solution(mesh):
     return jax.shard_map(
         shards,

time: 423 us -> 157 us (0.37)
  waiting for transfers between devices: 143 us -> 0.02 us
  Pallas kernels: 0 us -> 134 us
  other arithmetic: 129 us -> 0.6 us
  local copies, waits for them, and re-layouts: 104 us -> 4.42 us
  matrix products: 17.5 us -> 0 us
  blocking collectives: 16.3 us -> 0 us
    pallas_call x0 -> x9, Pallas kernels: none -> 134 us  [the longest x3 41.3 us: predict(): pl.pallas_call(functools.partial(predict_body, k, slot, before is not Non...]
    ppermute x2 -> x6, waiting for transfers between devices: 125 us -> 0.02 us  [from_behind(): lax.ppermute(value, axis, [(source, source + steps) for source in range(i...]
    scatter-add x1 -> x0, other arithmetic: 94.1 us -> none  [shards(): jax.ops.segment_sum(contrib.reshape(-1, width), flat.reshape(-1), num_seg...]
    gather x1 -> x0, local copies, waits for them, and re-layouts: 59.7 us -> none  [shards(): picked = joined[flat]]
    slice x4 -> x1, local copies, waits for them, and re-layouts: 30.9 us -> 1.19 us  [shards(): bad[2, 0] > 0]
    mul x3 -> x0, other arithmetic: 19.5 us -> none  [the longest x1 13.1 us: shards(): scaled = prior_std * adjoint]
    ppermute x2 -> x0, waiting for transfers between devices: 17.8 us -> none  [the longest x1 11.3 us: extended(): lax.ppermute(head, axis, [((i + 1) % count, i) for i in range(ends)])]
    dot_general x1 -> x0, matrix products: 17.5 us -> none  [shards(): jnp.dot(kernel, rim, preferred_element_type=jnp.float32, precision=lax.Pr...]
  transfers between devices with their start and end apart: 4 -> 6, of which waited for: 4 -> 0; matrix products, arithmetic and copies ran while one was open for 3% -> 0% of each run, Pallas kernels for 0% -> 43%
where the time goes in v1:
time: 157 us; the launch traced here: 156 us
  Pallas kernels  134 us (85%)
  starting transfers between devices  16.2 us (10%)
  local copies, waits for them, and re-layouts  4.42 us (3%)
    pallas_call x3, Pallas kernels, predict(): pl.pallas_call(functools.partial(predict_body, k, slot, before is not Non...  41.3 us
    pallas_call x2, Pallas kernels, sort_half(): pl.pallas_call(functools.partial(sort_body, nobs, which, hb), out_shape=(...  36.2 us
    pallas_call x1, Pallas kernels, exchange(): pl.pallas_call(exchange_body, grid=(1,), out_shape=(jax.ShapeDtypeStruct(...  21.7 us
    pallas_call x1, Pallas kernels, inner(): pl.pallas_call(inner_body, grid=(1,), out_shape=jax.ShapeDtypeStruct(ps.s...  19.2 us
    ppermute x6, starting transfers between devices, from_behind(): lax.ppermute(value, axis, [(source, source + steps) for source in range(i...  16.2 us
    pallas_call x1, Pallas kernels, edges(): pl.pallas_call(edges_body, grid=(1,), out_shape=(jax.ShapeDtypeStruct((KH...  9.24 us
    pallas_call x1, Pallas kernels, finish(): pl.pallas_call(finish_body, grid=(2, cells // wide), out_shape=jax.ShapeD...  6.59 us
  transfers between devices with their start and end apart: 6, of which 0 were waited for; matrix products, arithmetic and copies ran while one was open for 0% of the time, Pallas kernels for 43%

profile of v1, /device:TPU:1, one launch (start us, length us, event | category | flops | bytes accessed | tf_op | source)
XLA Modules:
  0.0 156.4 jit_solution(17847236914113666557)
XLA Ops:
  0.0 0.0 copy-start.14
  0.0 0.0 copy-start.13
  0.0 0.0 copy-start.4
  0.0 18.2 %sort_half.2 = (bf16[5248,128]{1,0:T(8,128)(2,1)S(1)}, bf16[5248,128]{1,0:T(8,128)(2,1)S(1)}, s32[136,128]{1,0:T(8,128)S(1)}, s32[136,128]{1,0:T(8,128)S(1)}) custom-call(s32[1,1024]{1,0:T(1,128)} %bitcast.21, s32[16,1024]{1,0:T(8,128)} %bitcast.17, s32[16,1024]{1,0:T(8,128)} %bitcast.19, bf16[16384,128]{1,0:T(8,128)(2,1)} %bitcast.13), custom_call_target="tpu_custom_call" | custom-call | flops 1000000000 | bytes 52428800 | tf_op jit(solution)/shard_map/sort_half/pallas_call | solution.py:275
  18.2 3.3 %collective-permute-start.8 = (bf16[5248,128]{1,0:T(8,128)(2,1)S(1)}, bf16[5248,128]{1,0:T(8,128)(2,1)S(1)}, u32[]{:S(2)}, u32[]{:S(2)}) collective-permute-start(bf16[5248,128]{1,0:T(8,128)(2,1)S(1)} %get-tuple-element.83), channel_id=1, source_target_pairs={{8,0},{16,8},{24,16},{32,24},{40,32},{48,40},{56,48},{64,56},{72,6... | collective-permute-start | bytes 4030472 | tf_op jit(solution)/shard_map/ppermute | solution.py:47
  21.5 18.0 %sort_half.3 = (bf16[5248,128]{1,0:T(8,128)(2,1)S(1)}, bf16[5248,128]{1,0:T(8,128)(2,1)S(1)}, s32[136,128]{1,0:T(8,128)S(1)}, s32[136,128]{1,0:T(8,128)S(1)}) custom-call(s32[1,1024]{1,0:T(1,128)} %bitcast.22, s32[16,1024]{1,0:T(8,128)} %bitcast.18, s32[16,1024]{1,0:T(8,128)} %bitcast.20, bf16[16384,128]{1,0:T(8,128)(2,1)} %bitcast.14), custom_call_target="tpu_custom_call" | custom-call | flops 1000000000 | bytes 52428800 | tf_op jit(solution)/shard_map/sort_half/pallas_call | solution.py:275
  39.5 0.0 copy-start.5
  39.5 1.9 %collective-permute-start.6 = (bf16[5248,128]{1,0:T(8,128)(2,1)S(1)}, bf16[5248,128]{1,0:T(8,128)(2,1)S(1)}, u32[]{:S(2)}, u32[]{:S(2)}) collective-permute-start(bf16[5248,128]{1,0:T(8,128)(2,1)S(1)} %get-tuple-element.81), channel_id=1, source_target_pairs={{8,0},{16,8},{24,16},{32,24},{40,32},{48,40},{56,48},{64,56},{72,6... | collective-permute-start | bytes 4030472 | tf_op jit(solution)/shard_map/ppermute | solution.py:47
  41.4 1.9 %collective-permute-start.7 = (s32[136,128]{1,0:T(8,128)S(1)}, s32[136,128]{1,0:T(8,128)S(1)}, u32[]{:S(2)}, u32[]{:S(2)}) collective-permute-start(s32[136,128]{1,0:T(8,128)S(1)} %get-tuple-element.82), channel_id=1, source_target_pairs={{8,0},{16,8},{24,16},{32,24},{40,32},{48,40},{56,48},{64,56},{72,6... | collective-permute-start | bytes 208904 | tf_op jit(solution)/shard_map/ppermute | solution.py:47
  43.4 1.9 %collective-permute-start.9 = (s32[136,128]{1,0:T(8,128)S(1)}, s32[136,128]{1,0:T(8,128)S(1)}, u32[]{:S(2)}, u32[]{:S(2)}) collective-permute-start(s32[136,128]{1,0:T(8,128)S(1)} %get-tuple-element.84), channel_id=1, source_target_pairs={{8,0},{16,8},{24,16},{32,24},{40,32},{48,40},{56,48},{64,56},{72,6... | collective-permute-start | bytes 208904 | tf_op jit(solution)/shard_map/ppermute | solution.py:47
  45.3 0.0 copy-done.14
  45.3 0.0 copy-done.13
  45.3 0.6 pad_maximum_fusion.1.obs_ref
  45.9 0.0 copy-done.4
  45.9 0.0 copy-start.10
  45.9 0.0 copy-start.11
  45.9 0.0 copy-start.12
  45.9 17.9 %predict.3.own_ref = f32[8,128]{1,0:T(8,128)S(1)} custom-call(bf16[240,8192]{1,0:T(8,128)(2,1)S(1)} %copy-done.4, bf16[5248,128]{1,0:T(8,128)(2,1)S(1)} %get-tuple-element.77.refs_1_, bf16[5248,128]{1,0:T(8,128)(2,1)S(1)} %get-tuple-element.78.refs_2_, s32[136,128]{1,0:T(8,128)S(1)} %get-tuple-element.79.refs_3_.refs_5_.tab0_ref, ...), custom_call_target="tpu_custom_call" | custom-call | flops 1006632960 | bytes 20971520 | tf_op jit(solution)/shard_map/predict/pallas_call | solution.py:357
  63.8 0.0 copy-start.1
  63.8 0.6 copy-done.1
  64.4 0.0 collective-permute-done.9.refs_2_.refs_3_
  64.4 0.0 collective-permute-done.8.refs_1_
  64.4 11.7 %predict.4.refs_4_ = f32[8,128]{1,0:T(8,128)S(1)} custom-call(bf16[240,8192]{1,0:T(8,128)(2,1)S(1)} %copy-done.4, bf16[5248,128]{1,0:T(8,128)(2,1)S(1)} %collective-permute-done.8.refs_1_, s32[136,128]{1,0:T(8,128)S(1)} %collective-permute-done.9.refs_2_.refs_3_, s32[136,128]{1,0:T(8,128)S(1)} %collective-permute-done.9.refs_2_.refs_3_), custom_call_target="tpu_custom_call" | custom-call | flops 503316480 | bytes 15728640 | tf_op jit(solution)/shard_map/predict/pallas_call | solution.py:357
  76.1 0.0 collective-permute-done.7.refs_2_.refs_3_
  76.1 0.0 collective-permute-done.6.refs_1_
  76.1 0.0 copy-done.5
  76.1 0.0 copy-start.7
  76.1 1.1 copy-done.7
  77.2 11.7 %predict.5.next_ref = f32[8,128]{1,0:T(8,128)S(1)} custom-call(bf16[240,8192]{1,0:T(8,128)(2,1)S(1)} %copy-done.4, bf16[5248,128]{1,0:T(8,128)(2,1)S(1)} %collective-permute-done.6.refs_1_, s32[136,128]{1,0:T(8,128)S(1)} %collective-permute-done.7.refs_2_.refs_3_, s32[136,128]{1,0:T(8,128)S(1)} %collective-permute-done.7.refs_2_.refs_3_, ...), custom_call_target="tpu_custom_call" | custom-call | flops 503316480 | bytes 15728640 | tf_op jit(solution)/shard_map/predict/pallas_call | solution.py:357
  88.9 0.0 copy-start.2
  88.9 0.6 copy-done.2
  89.5 21.7 %exchange.1 = (f32[2,8,128]{2,1,0:T(8,128)S(1)}, s32[8,128]{1,0:T(8,128)}) custom-call(f32[8,128]{1,0:T(8,128)} %copy-done.1, f32[8,128]{1,0:T(8,128)} %copy-done.2, f32[2,8,128]{2,1,0:T(8,128)} %pad_maximum_fusion.1.obs_ref, s32[136,128]{1,0:T(8,128)S(1)} %get-tuple-element.79.refs_3_.refs_5_.tab0_ref, s32[136,128]{1,0:T(8,128)S(1)} %get-tuple-element.80.refs_4_.refs_6_.tab1_ref), custom_call_target="tpu_custom_call" | custom-call | tf_op jit(solution)/shard_map/exchange/pallas_call | solution.py:527
  111.2 1.2 slice.21
  113.1 0.0 copy-done.10
  113.1 0.0 copy-done.11
  113.1 0.0 copy-done.12
  113.1 43.3 %conditional.1 = (f32[240,8192]{1,0:T(8,128)}) conditional(s32[]{:T(128)} %bitcast.11, (f32[2,8,128]{2,1,0:T(8,128)S(1)}, f32[240,8192]{1,0:T(8,128)}, bf16[5248,128]{1,0:T(8,128)(2,1)S(1)}, bf16[5248,128]{1,0:T(8,128)(2,1)}, bf16[5248,128]{1,0:T(8,128)(2,1)S(1)}, /*index=5*/bf16[5248,128]{1,0:T(8,128)(2,1)}, s32[136,128]{1,0:T(8,128)S(1)}, ...), branch_computations={%region_0.0_spmd, %region_1.4_spmd} | conditional | flops 6836399616 | bytes 253735552 | solution.py:762
  113.1 0.0 copy-start
  113.1 0.0 copy-start.3
  113.1 0.0 copy-start.6
  113.1 0.0 copy-start.8
  113.1 9.2 %edges.1 = (f32[24,8192]{1,0:T(8,128)S(1)}, f32[24,8192]{1,0:T(8,128)S(1)}) custom-call(f32[2,8,128]{2,1,0:T(8,128)S(1)} %get-tuple-element.46.w_ref, f32[240,8192]{1,0:T(8,128)} %get-tuple-element.47.ps_head.ps_tail.ps_ref, f32[240,8192]{1,0:T(8,128)} %get-tuple-element.47.ps_head.ps_tail.ps_ref, bf16[5248,128]{1,0:T(8,128)(2,1)S(1)} %get-tuple-element.48.refs_0_, ...), custom_call_target="tpu_custom_call" | custom-call | flops 100000000 | bytes 8388608 | tf_op jit(solution)/shard_map/cond/branch_0_fun/edges/pallas_call | solution.py:594
  122.4 3.9 %collective-permute-start.1 = (f32[24,8192]{1,0:T(8,128)S(1)}, f32[24,8192]{1,0:T(8,128)S(1)}, u32[]{:S(2)}, u32[]{:S(2)}) collective-permute-start(f32[24,8192]{1,0:T(8,128)S(1)} %get-tuple-element.56.head_ref), channel_id=1, source_target_pairs={{8,0},{16,8},{24,16},{32,24},{40,32},{48,40},{56,48},{64,56},{72,6... | collective-permute-start | bytes 2359304 | tf_op jit(solution)/shard_map/cond/branch_0_fun/ppermute | solution.py:47
  126.3 3.2 %collective-permute-start = (f32[24,8192]{1,0:T(8,128)S(1)}, f32[24,8192]{1,0:T(8,128)}, u32[]{:S(2)}, u32[]{:S(2)}) collective-permute-start(f32[24,8192]{1,0:T(8,128)S(1)} %get-tuple-element.57.tail_ref), channel_id=1, source_target_pairs={{0,8},{8,16},{16,24},{24,32},{32,40},{40,48},{48,56},{56,64},{64,7... | collective-permute-start | bytes 2359304 | tf_op jit(solution)/shard_map/cond/branch_0_fun/ppermute | solution.py:47
  129.6 0.0 copy-done
  129.6 0.0 copy-done.3
  129.6 0.0 copy-done.6
  129.6 0.0 copy-done.8
  129.6 19.2 %inner.1.own_ref = f32[240,8192]{1,0:T(8,128)} custom-call(f32[2,8,128]{2,1,0:T(8,128)S(1)} %get-tuple-element.46.w_ref, f32[24,8192]{1,0:T(8,128)S(1)} %get-tuple-element.56.head_ref, f32[24,8192]{1,0:T(8,128)S(1)} %get-tuple-element.57.tail_ref, bf16[240,768]{1,0:T(8,128)(2,1)S(1)} %copy-done, f32[240,8192]{1,0:T(8,128)S(1)} %copy-done.3, ...), custom_call_target="tpu_custom_call" | custom-call | flops 4000000000 | bytes 41943040 | tf_op jit(solution)/shard_map/cond/branch_0_fun/inner/pallas_call | solution.py:673
  148.8 0.0 collective-permute-done.1.below_ref
  148.8 0.0 copy-start.9
  148.9 0.9 copy-done.9
  149.8 0.0 collective-permute-done.above_ref
  149.8 6.6 %finish.1 = f32[240,8192]{1,0:T(8,128)} custom-call(f32[240,8192]{1,0:T(8,128)} %inner.1.own_ref, f32[240,8192]{1,0:T(8,128)} %get-tuple-element.47.ps_head.ps_tail.ps_ref, f32[24,8192]{1,0:T(8,128)} %collective-permute-done.above_ref, f32[24,8192]{1,0:T(8,128)} %copy-done.9), custom_call_target="tpu_custom_call", output_to_operand_aliasing={{}: (0, {})} | custom-call | tf_op jit(solution)/shard_map/cond/branch_0_fun/finish/pallas_call | solution.py:715
Async XLA Ops:
  0.0 45.3 %copy-start.14 = (f32[1024]{0:T(1024)S(1)}, f32[1024]{0:T(1024)}, u32[]{:S(2)}) copy-start(f32[1024]{0:T(1024)} %param.14) | copy-start | bytes 12292
  0.0 45.3 %copy-start.13 = (f32[1024]{0:T(1024)S(1)}, f32[1024]{0:T(1024)}, u32[]{:S(2)}) copy-start(f32[1024]{0:T(1024)} %param.15) | copy-start | bytes 12292
  0.0 45.9 %copy-start.4 = (bf16[240,8192]{1,0:T(8,128)(2,1)S(1)}, bf16[240,8192]{1,0:T(8,128)(2,1)}, u32[]{:S(2)}) copy-start(bf16[240,8192]{1,0:T(8,128)(2,1)} %refs_0_.5) | copy-start | bytes 11796484
  18.2 46.2 %collective-permute-start.8 = (bf16[5248,128]{1,0:T(8,128)(2,1)S(1)}, bf16[5248,128]{1,0:T(8,128)(2,1)S(1)}, u32[]{:S(2)}, u32[]{:S(2)}) collective-permute-start(bf16[5248,128]{1,0:T(8,128)(2,1)S(1)} %get-tuple-element.83), channel_id=1, source_target_pairs={{8,0},{16,8},{24,16},{32,24},{40,32},{48,40},{56,48},{64,56},{72,6... | collective-permute-start | bytes 4030472 | tf_op jit(solution)/shard_map/ppermute | solution.py:47
  39.5 36.6 %copy-start.5 = (bf16[5248,128]{1,0:T(8,128)(2,1)}, bf16[5248,128]{1,0:T(8,128)(2,1)S(1)}, u32[]{:S(2)}) copy-start(bf16[5248,128]{1,0:T(8,128)(2,1)S(1)} %get-tuple-element.78.refs_2_) | copy-start | bytes 4030468
  39.5 36.6 %collective-permute-start.6 = (bf16[5248,128]{1,0:T(8,128)(2,1)S(1)}, bf16[5248,128]{1,0:T(8,128)(2,1)S(1)}, u32[]{:S(2)}, u32[]{:S(2)}) collective-permute-start(bf16[5248,128]{1,0:T(8,128)(2,1)S(1)} %get-tuple-element.81), channel_id=1, source_target_pairs={{8,0},{16,8},{24,16},{32,24},{40,32},{48,40},{56,48},{64,56},{72,6... | collective-permute-start | bytes 4030472 | tf_op jit(solution)/shard_map/ppermute | solution.py:47
  41.4 34.7 %collective-permute-start.7 = (s32[136,128]{1,0:T(8,128)S(1)}, s32[136,128]{1,0:T(8,128)S(1)}, u32[]{:S(2)}, u32[]{:S(2)}) collective-permute-start(s32[136,128]{1,0:T(8,128)S(1)} %get-tuple-element.82), channel_id=1, source_target_pairs={{8,0},{16,8},{24,16},{32,24},{40,32},{48,40},{56,48},{64,56},{72,6... | collective-permute-start | bytes 208904 | tf_op jit(solution)/shard_map/ppermute | solution.py:47
  43.4 21.0 %collective-permute-start.9 = (s32[136,128]{1,0:T(8,128)S(1)}, s32[136,128]{1,0:T(8,128)S(1)}, u32[]{:S(2)}, u32[]{:S(2)}) collective-permute-start(s32[136,128]{1,0:T(8,128)S(1)} %get-tuple-element.84), channel_id=1, source_target_pairs={{8,0},{16,8},{24,16},{32,24},{40,32},{48,40},{56,48},{64,56},{72,6... | collective-permute-start | bytes 208904 | tf_op jit(solution)/shard_map/ppermute | solution.py:47
  45.9 67.2 %copy-start.10 = (s32[1024,16]{0,1:T(8,128)S(1)}, s32[1024,16]{0,1:T(8,128)}, u32[]{:S(2)}) copy-start(s32[1024,16]{0,1:T(8,128)} %param.17) | copy-start | bytes 196612
  45.9 67.2 %copy-start.11 = (s32[1024,16]{0,1:T(8,128)S(1)}, s32[1024,16]{0,1:T(8,128)}, u32[]{:S(2)}) copy-start(s32[1024,16]{0,1:T(8,128)} %param.18) | copy-start | bytes 196612
  45.9 67.2 %copy-start.12 = (s32[1024]{0:T(1024)S(1)}, s32[1024]{0:T(1024)}, u32[]{:S(2)}) copy-start(s32[1024]{0:T(1024)} %param.16) | copy-start | bytes 12292
  63.8 0.6 copy-start.1
  76.1 1.1 copy-start.7
  88.9 0.6 copy-start.2
  113.1 16.5 %copy-start = (bf16[240,768]{1,0:T(8,128)(2,1)S(1)}, bf16[240,768]{1,0:T(8,128)(2,1)}, u32[]{:S(2)}) copy-start(bf16[240,768]{1,0:T(8,128)(2,1)} %constant.25.clone.1.kern_ref) | copy-start | bytes 1105924 | tf_op jit(solution)/shard_map/cond
  113.1 16.5 %copy-start.3 = (f32[240,8192]{1,0:T(8,128)S(1)}, f32[240,8192]{1,0:T(8,128)}, u32[]{:S(2)}) copy-start(f32[240,8192]{1,0:T(8,128)} %get-tuple-element.47.ps_head.ps_tail.ps_ref) | copy-start | bytes 23592964 | tf_op jit(solution)/shard_map/cond
  113.1 16.5 %copy-start.6 = (bf16[5248,128]{1,0:T(8,128)(2,1)S(1)}, bf16[5248,128]{1,0:T(8,128)(2,1)}, u32[]{:S(2)}) copy-start(bf16[5248,128]{1,0:T(8,128)(2,1)} %get-tuple-element.49.refs_1_) | copy-start | bytes 4030468 | tf_op jit(solution)/shard_map/cond
  113.1 16.5 %copy-start.8 = (bf16[5248,128]{1,0:T(8,128)(2,1)S(1)}, bf16[5248,128]{1,0:T(8,128)(2,1)}, u32[]{:S(2)}) copy-start(bf16[5248,128]{1,0:T(8,128)(2,1)} %get-tuple-element.51.refs_3_) | copy-start | bytes 4030468 | tf_op jit(solution)/shard_map/cond
  122.4 26.4 %collective-permute-start.1 = (f32[24,8192]{1,0:T(8,128)S(1)}, f32[24,8192]{1,0:T(8,128)S(1)}, u32[]{:S(2)}, u32[]{:S(2)}) collective-permute-start(f32[24,8192]{1,0:T(8,128)S(1)} %get-tuple-element.56.head_ref), channel_id=1, source_target_pairs={{8,0},{16,8},{24,16},{32,24},{40,32},{48,40},{56,48},{64,56},{72,6... | collective-permute-start | bytes 2359304 | tf_op jit(solution)/shard_map/cond/branch_0_fun/ppermute | solution.py:47
  126.3 23.5 %collective-permute-start = (f32[24,8192]{1,0:T(8,128)S(1)}, f32[24,8192]{1,0:T(8,128)}, u32[]{:S(2)}, u32[]{:S(2)}) collective-permute-start(f32[24,8192]{1,0:T(8,128)S(1)} %get-tuple-element.57.tail_ref), channel_id=1, source_target_pairs={{0,8},{8,16},{16,24},{24,32},{32,40},{40,48},{48,56},{56,64},{64,7... | collective-permute-start | bytes 2359304 | tf_op jit(solution)/shard_map/cond/branch_0_fun/ppermute | solution.py:47
  148.8 0.9 copy-start.9

commit v2 on v1

v2 whole, which is shorter than its diff:
```python
import functools

import jax
import jax.numpy as jnp
import numpy as np
from jax import lax
from jax.experimental import pallas as pl
from jax.experimental.pallas import tpu as pltpu
from jax.sharding import PartitionSpec as P

KH = 24
LANES = 128
CELLS = 64
NBIN = 2 * CELLS
HEAD = 41 * LANES
NEAR = 32
META = CELLS + CELLS + 8
F32, BF16, I32 = jnp.float32, jnp.bfloat16, jnp.int32
NT = (((1,), (1,)), ((), ()))
MESH = pl.DeviceIdType.MESH
VM = pl.BlockSpec(memory_space=pltpu.VMEM)
HBM = pl.BlockSpec(memory_space=pltpu.HBM)
TAB = pl.BlockSpec((8, LANES), lambda *_: (META // 8 - 1, 0), memory_space=pltpu.SMEM)
TABV = pl.BlockSpec((8, LANES), lambda *_: (META // 8 - 1, 0))


def iota(shape, dim):
    return lax.broadcasted_iota(I32, shape, dim)


def dot(a, b):
    return jnp.dot(a, b, preferred_element_type=F32)


def halves(v):
    top = v.astype(BF16).astype(F32)
    return top, v - top


def pick(table, lane):
    return jnp.take_along_axis(table, jnp.broadcast_to(lane, table.shape), axis=1, mode="promise_in_bounds")


def from_behind(value, axis, steps):
    count = lax.axis_size(axis)
    initial, last = (max(0, -steps), min(count, count - steps))
    return lax.ppermute(value, axis, [(source, source + steps) for source in range(initial, last)])


def extended(cells, sides, width):
    for axis, dim in sides:
        count = lax.axis_size(axis)
        ends = count - 1
        head = lax.slice_in_dim(cells, 0, width, axis=dim)
        tail = lax.slice_in_dim(cells, cells.shape[dim] - width, cells.shape[dim], axis=dim)
        cells = jnp.concatenate(
            [
                lax.ppermute(tail, axis, [(i, (i + 1) % count) for i in range(ends)]),
                cells,
                lax.ppermute(head, axis, [((i + 1) % count, i) for i in range(ends)]),
            ],
            axis=dim,
        )
    return cells


def misfits(partial_value, obs_value, obs_weight):
    predicted = lax.psum(partial_value, "tile")
    return (predicted - obs_value) * obs_weight


def general(flux, prior_std, footprint, obs_value, obs_weight, obs_hour, hour_offset, block_cell):
    hours = flux.shape[0]
    cells = flux.shape[1]
    width = footprint.shape[2]
    per_hour = cells // width
    earlier = from_behind(flux, "win", 1)
    joined = jnp.concatenate([earlier, flux], axis=0).reshape(2 * hours * per_hour, width)
    flat = (hours + obs_hour[:, None] - hour_offset) * per_hour + block_cell
    picked = joined[flat]
    partial_value = jnp.einsum("onc,onc->o", footprint, picked, preferred_element_type=jnp.float32)
    weighted = misfits(partial_value, obs_value, obs_weight)
    contrib = weighted[:, None, None] * footprint.astype(jnp.float32)
    summed = jax.ops.segment_sum(
        contrib.reshape(-1, width), flat.reshape(-1), num_segments=2 * hours * per_hour
    )
    summed = summed.reshape(2 * hours, cells)
    returned = from_behind(summed[:hours], "win", -1)
    adjoint = summed[hours:] + returned
    scaled = prior_std * adjoint
    rim = extended(scaled, (("win", 0),), KH)
    rows = jnp.arange(hours, dtype=jnp.int32)[:, None]
    columns = jnp.arange(hours + 2 * KH, dtype=jnp.int32)[None, :]
    distance = columns - rows - KH
    kernel = jnp.where(
        jnp.abs(distance) <= KH, jnp.exp(-2.0 * jnp.abs(distance).astype(jnp.float32) / KH), 0.0
    )
    smoothed = jnp.dot(
        kernel, rim, preferred_element_type=jnp.float32, precision=lax.Precision.HIGHEST
    )
    return prior_std * smoothed


def sort_body(nobs, which, hb, oh_ref, off_ref, cell_ref, fp_ref, own_ref, neg_ref, ometa_ref, nmeta_ref,
              fpv, stage, rows, keyv, hourv, posv, poss, tabs, tabv, sems):
    nblk = off_ref.shape[0]
    n = nobs * nblk
    per = nobs // LANES
    lines = nblk * per
    cap = n + CELLS * 16 + LANES
    span = HEAD // LANES - 1
    outs, metas = (own_ref, neg_ref), (ometa_ref, nmeta_ref)
    fetch = pltpu.make_async_copy(fp_ref.at[pl.ds(which * n, n)], fpv, sems.at[0])
    fetch.start()
    bins = iota((NBIN, LANES), 0)
    lanes = iota((NBIN, LANES), 1)
    upper = (bins < lanes).astype(BF16)
    ones = jnp.ones((LANES, LANES), BF16)
    same = (bins // CELLS) == (lanes // CELLS)
    below = jnp.where(same & (lanes < bins), 1.0, 0.0).astype(BF16)
    before = jnp.where(same & (bins < lanes), 1.0, 0.0).astype(BF16)

    for c in range(per):
        cut = slice(which * nobs + c * LANES, which * nobs + (c + 1) * LANES)
        hour = oh_ref[:, cut] - off_ref[:, cut]
        early = hour < 0
        hour = jnp.where(early, hour + hb, hour)
        key = jnp.where(early, cell_ref[:, cut] + CELLS, cell_ref[:, cut])
        rim = (hour < KH) | (hour >= hb - KH)
        at = slice(c * nblk, (c + 1) * nblk)
        keyv[0, at, :] = jnp.where(rim, key, -1)
        keyv[1, at, :] = jnp.where(rim, -1, key)
        keyv[2, at, :] = key
        hourv[at, :] = (hour + 1).astype(F32)

    def count(r, total):
        first, second = total
        for u in range(4):
            first = first + jnp.where(bins == keyv[0, pl.ds(r * 4 + u, 1), :], 1.0, 0.0)
            second = second + jnp.where(bins == keyv[1, pl.ds(r * 4 + u, 1), :], 1.0, 0.0)
        return first, second

    zero = jnp.zeros((NBIN, LANES), F32)
    first, second = lax.fori_loop(0, lines // 4, count, (zero, zero))
    first, second = first.astype(BF16), second.astype(BF16)
    ahead = [dot(v, upper) for v in (first, second)]
    rim_s = dot(first, ones)
    cnt_s = rim_s + dot(second, ones)
    rim_l = lax.dot_general(ones[:8], first, NT, preferred_element_type=F32)
    cnt_l = rim_l + lax.dot_general(ones[:8], second, NT, preferred_element_type=F32)

    def starts(cnt, left):
        tiles = jnp.floor((cnt + 15.0) * (1.0 / 16.0))
        coarse = jnp.floor(tiles * (1.0 / 128.0))
        fine = tiles - 128.0 * coarse

        def run(v):
            return dot(below, v.astype(BF16)) if left else dot(v.astype(BF16), before)

        return 16.0 * (128.0 * run(coarse) + run(fine))

    tight_l = starts(cnt_l, False)
    base = starts(cnt_s, True) + jnp.where(bins >= CELLS, float(cap), 0.0)
    line8 = iota((8, LANES), 0)
    limit = float(span * LANES)
    far = jnp.where((cnt_l > float(LANES)) | (rim_l > float(NEAR)) | (tight_l + cnt_l > limit), 1.0, 0.0)
    over = jnp.max(far, axis=1, keepdims=True)
    tab = jnp.where(line8 == 0, jnp.minimum(cnt_l, float(LANES)),
                    jnp.where(line8 == 1, jnp.minimum(tight_l, limit), over)).astype(I32)
    tabv[...] = tab
    metas[0][2 * CELLS:META, :] = tab
    metas[1][2 * CELLS:META, :] = pltpu.roll(tab, CELLS, 1)
    to_tab = pltpu.make_async_copy(tabv, tabs, sems.at[1])
    to_tab.start()

    for turn in range(2):
        def place(r, acc):
            for u in range(4):
                at = pl.ds(r * 4 + u, 1)
                hot = bins == keyv[turn, at, :]
                posf = jnp.sum(jnp.where(hot, acc, 0.0), axis=0, keepdims=True).astype(I32)
                posv[at, :] = posf if turn == 0 else posv[at, :] + posf
                acc = jnp.where(hot, acc + 1.0, acc)
            return acc

        lax.fori_loop(0, lines // 4, place, base + ahead[turn] + (rim_s if turn else 0.0))
    to_pos = pltpu.make_async_copy(posv, poss, sems.at[2])
    to_pos.start()
    starts_l = tight_l + jnp.where(iota((8, LANES), 1) >= CELLS, float(cap), 0.0)
    for g in range(lines // 8):
        at = slice(g * 8, (g + 1) * 8)
        key = keyv[2, at, :]
        rank = posv[at, :] - pick(starts_l, key).astype(I32)
        keyv[0, at, :] = rank
        spot = jnp.where(rank < LANES, (key & (CELLS - 1)) * LANES + rank, -1)
        metas[0][CELLS + g * 8:CELLS + (g + 1) * 8, :] = jnp.where(key < CELLS, spot, -1)
        metas[1][CELLS + g * 8:CELLS + (g + 1) * 8, :] = jnp.where(key < CELLS, -1, spot)

    obs = iota((1, LANES), 1).astype(F32)
    done = zero
    for c in range(per):
        def gather(r, acc):
            marks, spots = [], []
            for u in range(4):
                at = pl.ds(c * nblk + r * 4 + u, 1)
                hot = bins == keyv[2, at, :]
                marks.append(jnp.concatenate(
                    [jnp.where(hot, v, 0.0).astype(BF16) for v in (hourv[at, :], obs)], axis=0))
                spots.append(jnp.where(bins == keyv[0, at, :], 1.0, 0.0).astype(BF16))
            return acc + lax.dot_general(jnp.concatenate(marks, axis=1), jnp.concatenate(spots, axis=1), NT,
                                         preferred_element_type=F32)

        acc = lax.fori_loop(0, nblk // 4, gather, jnp.zeros((2 * NBIN, LANES), F32))
        hour, low = acc[:NBIN], acc[NBIN:]
        done = done + jnp.where(hour > 0.0, hour + 256.0 * (low + float(c * LANES)), 0.0)
    done = done.astype(I32)
    metas[0][0:CELLS, :] = done[:CELLS]
    metas[1][0:CELLS, :] = done[CELLS:]
    to_tab.wait()
    blocks = []
    for side in range(2):
        last = CELLS - 1 + CELLS * side
        end = jnp.minimum(tabs[1, last] + tabs[0, last], span * LANES)
        blocks.append(jnp.minimum(lax.shift_right_logical(end + 270, 7), span + 1))

    for side in range(2):
        def blank(i, _):
            at = pl.multiple_of(i * LANES + side * cap, LANES)
            rows[pl.ds(at, LANES), :] = jnp.zeros((LANES, LANES), F32)
            return 0

        lax.fori_loop(0, blocks[side], blank, 0)
    fetch.wait()

    def unpack(i, _):
        for u in range(8):
            at = pl.multiple_of(i * 128 + u * 16, 16)
            stage[pl.ds(at, 16), :] = fpv[pl.ds(at, 16), :].astype(F32)
        return 0

    lax.fori_loop(0, n // 128, unpack, 0)
    to_pos.wait()

    def permute(r, _):
        c = lax.shift_right_logical(r, 4)
        src = c * (LANES * nblk) + (r & 15)
        for l in range(LANES):
            rows[pl.ds(poss[r, l], 1), :] = stage[pl.ds(src + l * nblk, 1), :]
        return 0

    lax.fori_loop(0, lines, permute, 0)
    for side in range(2):
        def convert(i, _):
            at = pl.multiple_of(i * 128, 128)
            src = pl.multiple_of(at + side * cap, 128)
            outs[side][pl.ds(at, 128), :] = rows[pl.ds(src, 128), :].astype(BF16)
            return 0

        lax.fori_loop(0, blocks[side], convert, 0)


def sort_half(oh, off, cell, fp2, which, hb):
    nblk, count = off.shape
    nobs = count // 2
    n = nobs * nblk
    cap = n + CELLS * 16 + LANES
    lines = nblk * nobs // LANES
    return pl.pallas_call(
        functools.partial(sort_body, nobs, which, hb),
        out_shape=(jax.ShapeDtypeStruct((HEAD, LANES), BF16), jax.ShapeDtypeStruct((HEAD, LANES), BF16),
                   jax.ShapeDtypeStruct((META, LANES), I32), jax.ShapeDtypeStruct((META, LANES), I32)),
        in_specs=[VM, VM, VM, HBM],
        out_specs=(VM, VM, VM, VM),
        scratch_shapes=[
            pltpu.VMEM((n, LANES), BF16), pltpu.VMEM((n, LANES), F32), pltpu.VMEM((2 * cap, LANES), F32),
            pltpu.VMEM((3, lines, LANES), I32), pltpu.VMEM((lines, LANES), F32),
            pltpu.VMEM((lines, LANES), I32), pltpu.SMEM((lines, LANES), I32),
            pltpu.SMEM((8, LANES), I32),
            pltpu.VMEM((8, LANES), I32), pltpu.SemaphoreType.DMA((3,)),
        ],
        compiler_params=pltpu.CompilerParams(vmem_limit_bytes=24 << 20),
        cost_estimate=pl.CostEstimate(flops=10**9, bytes_accessed=50 << 20, transcendentals=0),
        name="sort_half",
    )(oh, off, cell, fp2)


def predict_body(k, slot, chained, *refs):
    flux_ref, rows, metas, tabs = refs[0], refs[1:1 + k], refs[1 + k:1 + 2 * k], refs[1 + 2 * k:1 + 3 * k]
    out_ref, tablev = refs[-2:]
    hours = iota((flux_ref.shape[0], k * LANES), 0) + 1
    step = 8

    def group(g, _):
        for u in range(step):
            b = g * step + u
            hour = jnp.concatenate([m[pl.ds(b, 1), :] & 255 for m in metas], axis=1)
            fp = jnp.concatenate(
                [rows[i][pl.ds(pl.multiple_of(tabs[i][1, b], 16), LANES), :] for i in range(k)], axis=0)
            local = flux_ref[:, pl.ds(pl.multiple_of(b * LANES, LANES), LANES)]
            full = lax.dot_general(local, fp, NT, preferred_element_type=F32)
            value = jnp.sum(jnp.where(hours == hour, full, 0.0), axis=0, keepdims=True)
            for i in range(k):
                tablev[i, pl.ds(b, 1), :] = value[:, i * LANES:(i + 1) * LANES]
        return 0

    lax.fori_loop(0, CELLS // step, group, 0)
    per = 4
    lines = []
    for i in range(k):
        spots = [metas[i][CELLS + g * 8:CELLS + (g + 1) * 8, :] for g in range(8)]
        cell = [lax.shift_right_arithmetic(s, 7) for s in spots]
        lane = [s & 127 for s in spots]

        def collect(q, acc):
            acc = list(acc)
            for u in range(4):
                b = q * 4 + u
                row = jnp.broadcast_to(tablev[i, pl.ds(b, 1), :], (8, LANES))
                for g in range(8):
                    acc[g // 2] = acc[g // 2] + jnp.where(cell[g] == b, pick(row, lane[g]), 0.0)
            return tuple(acc)

        acc = lax.fori_loop(0, CELLS // 4, collect, (jnp.zeros((8, LANES), F32),) * per)
        lines.append(jnp.concatenate([jnp.sum(a, axis=0, keepdims=True) for a in acc], axis=0))
    blank = jnp.zeros((per, LANES), F32)
    if k == 2:
        out_ref[...] = jnp.concatenate(lines, axis=0)
    elif not chained:
        out_ref[...] = jnp.concatenate([lines[0], blank], axis=0)
    else:
        mine_ref, other_ref, tab0_ref, tab1_ref = refs[1 + 3 * k:5 + 3 * k]
        out_ref[0] = mine_ref[...]
        out_ref[1] = jnp.concatenate([blank, lines[0]], axis=0) + other_ref[...]
        out_ref[2] = jnp.maximum(tab0_ref[...], tab1_ref[...]).astype(F32)


def predict(flux, pairs, slot=0, more=()):
    k = len(pairs)
    rows, metas = [r for r, _ in pairs], [m for _, m in pairs]
    return pl.pallas_call(
        functools.partial(predict_body, k, slot, len(more) > 0),
        grid=(1,),
        out_shape=jax.ShapeDtypeStruct((3, 8, LANES) if more else (8, LANES), F32),
        in_specs=[VM] + [VM] * k + [VM] * k + [TAB] * k + ([VM, VM, TABV, TABV] if more else []),
        out_specs=VM,
        scratch_shapes=[pltpu.VMEM((k, CELLS, LANES), F32)],
        compiler_params=pltpu.CompilerParams(vmem_limit_bytes=20 << 20),
        cost_estimate=pl.CostEstimate(flops=k * 2 * 240 * 8192 * 128, bytes_accessed=(10 + 5 * k) << 20,
                                      transcendentals=0),
        name="predict",
    )(flux, *rows, *metas, *metas, *more)


def exchange_body(p_ref, obs_ref, w_ref, bad_ref, pair, prev_n, next_o, next_obs, flags, mine,
                  s_pair, s_side, s_flag, r_pair, r_side, r_obs, r_flag):
    wins, tiles = lax.axis_size("win"), lax.axis_size("tile")
    w, t = lax.axis_index("win"), lax.axis_index("tile")
    up, down = w > 0, w < wins - 1
    barrier = pltpu.get_barrier_semaphore()
    peers = [lax.rem(t + d, tiles) for d in range(tiles)]
    others = [lax.rem(w + d, wins) for d in range(wins)]

    def greet(device):
        pl.semaphore_signal(barrier, inc=1, device_id=device, device_id_type=MESH)

    for d in range(1, tiles):
        greet((w, peers[d]))
    for d in range(1, wins):
        greet((others[d], t))

    @pl.when(up)
    def _():
        for d in range(1, tiles):
            greet((w - 1, peers[d]))

    @pl.when(down)
    def _():
        for d in range(1, tiles):
            greet((w + 1, peers[d]))

    sides = jnp.where(up, 1, 0) + jnp.where(down, 1, 0)
    pl.semaphore_wait(barrier, tiles - 1 + wins - 1 + sides * (tiles - 1))

    def push(src, dst, ssem, rsem, device):
        return pltpu.make_async_remote_copy(src_ref=src, dst_ref=dst, send_sem=ssem, recv_sem=rsem,
                                            device_id=device, device_id_type=MESH)

    def peer(d, at):
        return push(p_ref, pair.at[at], s_pair.at[d], r_pair.at[at], (w, peers[d]))

    def above(d, at):
        return push(p_ref.at[0], next_o.at[at], s_side.at[0, d], r_side.at[0, at], (w - 1, peers[d]))

    def under(d, at):
        return push(p_ref.at[1], prev_n.at[at], s_side.at[1, d], r_side.at[1, at], (w + 1, peers[d]))

    def obs_to(v):
        return push(obs_ref, next_obs, s_side.at[2, 0], r_obs, (v, t))

    def flag(d, at):
        return push(mine, flags.at[at], s_flag.at[d], r_flag.at[at], (others[d], t))

    for d in range(1, tiles):
        peer(d, t).start()

    @pl.when(up)
    def _():
        for d in range(tiles):
            above(d, t).start()
        obs_to(w - 1).start()

    @pl.when(down)
    def _():
        for d in range(tiles):
            under(d, t).start()

    own, later, bad = p_ref[0], p_ref[1], p_ref[2]
    for d in range(1, tiles):
        peer(d, peers[d]).wait_recv()
        got = pair.at[peers[d]]
        own, later, bad = own + got[0], later + got[1], jnp.maximum(bad, got[2])
    mine[...] = bad
    w_ref[0] = own
    w_ref[1] = later

    @pl.when(up)
    def _():
        total = w_ref[0]
        for d in range(tiles):
            under(d, peers[d]).wait_recv()
            total = total + prev_n[peers[d]]
        w_ref[0] = total

    w_ref[0] = (w_ref[0] - obs_ref[0]) * obs_ref[1]
    for d in range(1, wins):
        flag(d, w).start()

    @pl.when(down)
    def _():
        total = w_ref[1]
        for d in range(tiles):
            above(d, peers[d]).wait_recv()
            total = total + next_o[peers[d]]
        obs_to(w + 1).wait_recv()
        w_ref[1] = (total - next_obs[0]) * next_obs[1]

    for d in range(1, wins):
        flag(d, others[d]).wait_recv()
        bad = jnp.maximum(bad, flags[others[d]])
    bad_ref[...] = bad
    for d in range(1, wins):
        flag(d, w).wait_send()
    for d in range(1, tiles):
        peer(d, t).wait_send()

    @pl.when(up)
    def _():
        obs_to(w - 1).wait_send()
        for d in range(tiles):
            above(d, t).wait_send()

    @pl.when(down)
    def _():
        for d in range(tiles):
            under(d, t).wait_send()


def exchange(packet, obs):
    wins, tiles = lax.axis_size("win"), lax.axis_size("tile")
    block = pltpu.VMEM((tiles, 8, LANES), F32)
    sem = pltpu.SemaphoreType.DMA
    return pl.pallas_call(
        exchange_body,
        out_shape=(jax.ShapeDtypeStruct((2, 8, LANES), F32), jax.ShapeDtypeStruct((8, LANES), F32)),
        in_specs=[VM, VM],
        out_specs=(VM, VM),
        scratch_shapes=[pltpu.VMEM((tiles, 3, 8, LANES), F32), block, block, pltpu.VMEM((2, 8, LANES), F32),
                        pltpu.VMEM((wins, 8, LANES), F32), pltpu.VMEM((8, LANES), F32),
                        sem((tiles,)), sem((3, tiles)), sem((wins,)), sem((tiles,)), sem((2, tiles)), sem,
                        sem((wins,))],
        compiler_params=pltpu.CompilerParams(collective_id=3, has_side_effects=True),
        name="exchange",
    )(packet, obs)


def weigh(code, tables, slots):
    got = [pick(table, lax.shift_right_logical(code, 8) & 127) for table in tables]
    got = got[0] if len(got) == 1 else jnp.where(iota((8, LANES), 1) < 2 * NEAR, got[0], got[1])
    mine = iota((8, LANES), 0) == lax.shift_right_logical(code, 15) + slots
    return jnp.sum(jnp.where(mine, got, 0.0), axis=0, keepdims=True)


def spread(hour, hours, w):
    hit = hours == hour
    return [jnp.where(hit, v, 0.0).astype(BF16) for v in halves(w)]


def edges_body(w_ref, ps_head, ps_tail, *refs):
    rows, metas, tabs = refs[0:4], refs[4:8], refs[8:12]
    head_ref, tail_ref = refs[12:]
    total = 240
    band = iota((2 * KH, LANES), 0)
    hours = jnp.where(band < KH, band, band + (total - 2 * KH)) + 1
    quarter = lax.shift_right_logical(iota((1, LANES), 1), 5)
    slots = (quarter & 1) * 4
    tables = [w_ref[0], w_ref[1]]

    def group(g, _):
        for u in range(4):
            b = g * 4 + u
            code = metas[0][pl.ds(b, 1), :]
            fps = []
            for i in range(4):
                if i:
                    code = jnp.where(quarter == i, pltpu.roll(metas[i][pl.ds(b, 1), :], i * NEAR, 1), code)
                fps.append(rows[i][pl.ds(pl.multiple_of(tabs[i][1, b], 16), NEAR), :])
            fp = jnp.concatenate(fps, axis=0)
            left = jnp.concatenate(spread(code & 255, hours, weigh(code, tables, slots)), axis=1)
            part = dot(left, jnp.concatenate([fp, fp], axis=0))
            col = pl.ds(pl.multiple_of(b * LANES, LANES), LANES)
            head_ref[:, col] = part[:KH] * ps_head[:, col]
            tail_ref[:, col] = part[KH:] * ps_tail[:, col]
        return 0

    lax.fori_loop(0, CELLS // 4, group, 0)


def edges(w, ps, pairs):
    rows, metas = [r for r, _ in pairs], [m for _, m in pairs]
    cells = ps.shape[1]
    last = ps.shape[0] // KH - 1
    return pl.pallas_call(
        edges_body,
        grid=(1,),
        out_shape=(jax.ShapeDtypeStruct((KH, cells), F32), jax.ShapeDtypeStruct((KH, cells), F32)),
        in_specs=[VM, pl.BlockSpec((KH, cells), lambda *_: (0, 0)), pl.BlockSpec((KH, cells), lambda *_: (last, 0))]
        + [VM] * 4 + [VM] * 4 + [TAB] * 4,
        out_specs=(VM, VM),
        compiler_params=pltpu.CompilerParams(vmem_limit_bytes=20 << 20),
        cost_estimate=pl.CostEstimate(flops=10**8, bytes_accessed=8 << 20, transcendentals=0),
        name="edges",
    )(w, ps, ps, *rows, *metas, *metas)


def inner_body(w_ref, head_ref, tail_ref, kern_ref, ps_ref, *refs):
    rows, metas, tabs = refs[0:4], refs[4:8], refs[8:12]
    out_ref, outv, sv, osems = refs[12:]
    total, cells = ps_ref.shape
    parts = 16
    wide = cells // parts
    per = CELLS // parts
    inside = total - 2 * KH
    def drain(p):
        at = pl.ds(pl.multiple_of(p * wide, LANES), wide)
        return pltpu.make_async_copy(outv.at[p & 1], out_ref.at[:, at], osems.at[p & 1])

    hours = iota((inside, LANES), 0) + KH + 1
    pad = jnp.zeros((16, wide), BF16)

    def part_of(p, _):
        for u in range(per):
            b = p * per + u
            left, right = [], []
            for i in range(4):
                code = metas[i][pl.ds(b, 1), :]
                left += spread(code & 255, hours, weigh(code, [w_ref[i // 2]], (i % 2) * 4))
                fp = rows[i][pl.ds(pl.multiple_of(tabs[i][1, b], 16), LANES), :]
                right += [fp, fp]
            part = dot(jnp.concatenate(left, axis=1), jnp.concatenate(right, axis=0))
            col = pl.ds(pl.multiple_of(b * LANES, LANES), LANES)
            here = slice(u * LANES, (u + 1) * LANES)
            sv[:KH, here] = head_ref[:, col]
            sv[KH:total - KH, here] = part * ps_ref[KH:total - KH, col]
            sv[total - KH:, here] = tail_ref[:, col]
        top, low = halves(sv[...])
        top, low = top.astype(BF16), low.astype(BF16)
        stack = jnp.concatenate([top, pad, low, pad, top, pad], axis=0)
        smooth = dot(kern_ref[...], stack)

        @pl.when(p >= 2)
        def _():
            drain(p - 2).wait()

        outv[p & 1] = smooth * ps_ref[:, pl.ds(pl.multiple_of(p * wide, LANES), wide)]
        drain(p).start()
        return 0

    lax.fori_loop(0, parts, part_of, 0)
    for p in (parts - 2, parts - 1):
        drain(p).wait()


def inner(w, head, tail, kern, ps, pairs):
    rows, metas = [r for r, _ in pairs], [m for _, m in pairs]
    wide = ps.shape[1] // 16
    return pl.pallas_call(
        inner_body,
        grid=(1,),
        out_shape=jax.ShapeDtypeStruct(ps.shape, F32),
        in_specs=[VM, VM, VM, VM, VM] + [VM] * 4 + [VM] * 4 + [TAB] * 4,
        out_specs=HBM,
        scratch_shapes=[pltpu.VMEM((2, ps.shape[0], wide), F32), pltpu.VMEM((ps.shape[0], wide), F32),
                        pltpu.SemaphoreType.DMA((2,))],
        compiler_params=pltpu.CompilerParams(vmem_limit_bytes=32 << 20),
        cost_estimate=pl.CostEstimate(flops=4 * 10**9, bytes_accessed=40 << 20, transcendentals=0),
        name="inner",
    )(w, head, tail, kern, ps, *rows, *metas, *metas)


def finish_body(own_ref, ps_ref, above_ref, below_ref, out_ref, ownv, psv, halov, loads, stores):
    total = ps_ref.shape[0]
    row = iota((KH, LANES), 0).astype(F32)
    grow, decay = jnp.exp((row - KH) * (2.0 / KH)), jnp.exp(row * (-2.0 / KH))

    def fetch(side):
        at = pl.ds(side * (total - KH), KH)
        pieces = ((own_ref.at[at], ownv), (ps_ref.at[at], psv), ((above_ref, below_ref)[side], halov))
        return [pltpu.make_async_copy(src, dst.at[side], loads.at[side, i]) for i, (src, dst) in enumerate(pieces)]

    def store(side):
        return pltpu.make_async_copy(ownv.at[side], out_ref.at[pl.ds(side * (total - KH), KH)], stores.at[side])

    for side in range(2):
        for copy in fetch(side):
            copy.start()
    for side in range(2):
        for copy in fetch(side):
            copy.wait()
        scale, after = (grow, decay) if side == 0 else (decay, grow)

        def fill(q, _):
            for u in range(4):
                cut = pl.ds(pl.multiple_of((q * 4 + u) * LANES, LANES), LANES)
                x = halov[side, :, cut] * scale
                for s in (1, 2, 4, 8, 16):
                    gap = jnp.zeros((s, LANES), F32)
                    x = x + (jnp.concatenate([gap, x[:KH - s]], axis=0) if side
                             else jnp.concatenate([x[s:], gap], axis=0))
                ownv[side, :, cut] = ownv[side, :, cut] + psv[side, :, cut] * (x * after)
            return 0

        lax.fori_loop(0, ps_ref.shape[1] // LANES // 4, fill, 0)
        store(side).start()
    for side in range(2):
        store(side).wait()


def finish(partial, ps, above, below):
    band = pltpu.VMEM((2, KH, ps.shape[1]), F32)
    return pl.pallas_call(
        finish_body,
        out_shape=jax.ShapeDtypeStruct(ps.shape, F32),
        in_specs=[HBM] * 4,
        out_specs=HBM,
        scratch_shapes=[band, band, band, pltpu.SemaphoreType.DMA((2, 3)), pltpu.SemaphoreType.DMA((2,))],
        input_output_aliases={0: 0},
        name="finish",
    )(partial, ps, above, below)


def taps(distance):
    far = np.abs(distance)
    full = np.where(far <= KH, np.exp(np.float32(-2.0) * far.astype(np.float32) / np.float32(KH)), 0).astype(np.float32)
    top = full.astype(BF16)
    return top, (full - top.astype(np.float32)).astype(BF16)


def smoother(total):
    row, col = np.arange(total)[:, None], np.arange(256)[None, :]
    top, low = taps(np.where(col < total, row - col, total))
    return jnp.asarray(np.concatenate([top, top, low], axis=1))


def quick(flux, prior_std, w, pairs):
    head, tail = edges(w, prior_std, pairs)
    above = from_behind(tail, "win", 1)
    below = from_behind(head, "win", -1)
    partial = inner(w, head, tail, smoother(flux.shape[0]), prior_std, pairs)
    return finish(partial, prior_std, above, below)


def shards(flux, prior_std, footprint, obs_value, obs_weight, obs_hour, hour_offset, block_cell):
    count, nblk, width = footprint.shape
    own, theirs = [], []
    for k in range(2):
        rows, early, meta, early_meta = sort_half(
            obs_hour.reshape(1, count), hour_offset.T, block_cell.T,
            footprint.reshape(count * nblk, width), k, flux.shape[0])
        own.append((rows, meta))
        theirs.append((from_behind(early, "win", -1), from_behind(early_meta, "win", -1)))
    obs = jnp.stack([obs_value.reshape(8, LANES), obs_weight.reshape(8, LANES)])
    mine = predict(flux, own)
    other = predict(flux, theirs[:1])
    packet = predict(flux, theirs[1:], 1, (mine, other, own[0][1], own[1][1]))
    w, bad = exchange(packet, obs)
    return lax.cond(
        bad[2, 0] > 0.0,
        lambda: general(flux, prior_std, footprint, obs_value, obs_weight, obs_hour, hour_offset, block_cell),
        lambda: quick(flux, prior_std, w, own + theirs))


def solution(mesh):
    return jax.shard_map(
        shards,
        mesh=mesh,
        in_specs=(
            P("win", "tile"),
            P("win", "tile"),
            P("win", "tile", None),
            P("win"),
            P("win"),
            P("win"),
            P("win", "tile"),
            P("win", "tile"),
        ),
        out_specs=P("win", "tile"),
        check_vma=False,
    )
```

time: 157 us -> 135 us (0.86)
  Pallas kernels: 134 us -> 107 us
  waiting for transfers between devices: 0.02 us -> 5.84 us
    pallas_call x5, Pallas kernels: 69.6 us -> 46 us  [the longest x3 22.6 us: predict(): pl.pallas_call(functools.partial(predict_body, k, slot, len(more) > 0), g...]
    ppermute x6, waiting for transfers between devices: 0.02 us -> 5.84 us  [from_behind(): lax.ppermute(value, axis, [(source, source + steps) for source in range(i...]
    pallas_call x1, Pallas kernels: 9.24 us -> 7.44 us  [edges(): pl.pallas_call(edges_body, grid=(1,), out_shape=(jax.ShapeDtypeStruct((KH...]
  transfers between devices with their start and end apart: 6 -> 6, of which waited for: 0 -> 1; matrix products, arithmetic and copies ran while one was open for 0% -> 0% of each run, Pallas kernels for 43% -> 38%
where the time goes in v2:
time: 135 us; the launch traced here: 134 us
  Pallas kernels  107 us (79%)
  starting transfers between devices  16.1 us (12%)
  waiting for transfers between devices  5.84 us (4%)
  local copies, waits for them, and re-layouts  3.84 us (3%)
    pallas_call x2, Pallas kernels, sort_half(): pl.pallas_call(functools.partial(sort_body, nobs, which, hb), out_shape=(...  35.2 us
    pallas_call x3, Pallas kernels, predict(): pl.pallas_call(functools.partial(predict_body, k, slot, len(more) > 0), g...  22.6 us
    pallas_call x1, Pallas kernels, exchange(): pl.pallas_call(exchange_body, out_shape=(jax.ShapeDtypeStruct((2, 8, LANE...  19.6 us
    pallas_call x1, Pallas kernels, inner(): pl.pallas_call(inner_body, grid=(1,), out_shape=jax.ShapeDtypeStruct(ps.s...  17.9 us
    ppermute x6, starting transfers between devices, from_behind(): lax.ppermute(value, axis, [(source, source + steps) for source in range(i...  16.1 us
    pallas_call x1, Pallas kernels, edges(): pl.pallas_call(edges_body, grid=(1,), out_shape=(jax.ShapeDtypeStruct((KH...  7.44 us
    ppermute x6, waiting for transfers between devices, from_behind(): lax.ppermute(value, axis, [(source, source + steps) for source in range(i...  5.84 us
    pallas_call x1, Pallas kernels, finish(): pl.pallas_call(finish_body, out_shape=jax.ShapeDtypeStruct(ps.shape, F32)...  3.82 us
  transfers between devices with their start and end apart: 6, of which 1 were waited for; matrix products, arithmetic and copies ran while one was open for 0% of the time, Pallas kernels for 38%

profile of v2, /device:TPU:1, one launch (start us, length us, event | category | flops | bytes accessed | tf_op | source)
XLA Modules:
  0.0 134.2 jit_solution(10811867655039183770)
XLA Ops:
  0.0 0.0 copy-start.13
  0.0 0.0 copy-start.12
  0.0 0.0 copy-start.3
  0.0 17.7 %sort_half.3 = (bf16[5248,128]{1,0:T(8,128)(2,1)S(1)}, bf16[5248,128]{1,0:T(8,128)(2,1)S(1)}, s32[136,128]{1,0:T(8,128)S(1)}, s32[136,128]{1,0:T(8,128)S(1)}) custom-call(s32[1,1024]{1,0:T(1,128)} %bitcast.21, s32[16,1024]{1,0:T(8,128)} %bitcast.17, s32[16,1024]{1,0:T(8,128)} %bitcast.19, bf16[16384,128]{1,0:T(8,128)(2,1)} %bitcast.13), custom_call_target="tpu_custom_call" | custom-call | flops 1000000000 | bytes 52428800 | tf_op jit(solution)/shard_map/sort_half/pallas_call | solution.py:268
  17.7 3.3 %collective-permute-start.8 = (bf16[5248,128]{1,0:T(8,128)(2,1)S(1)}, bf16[5248,128]{1,0:T(8,128)(2,1)S(1)}, u32[]{:S(2)}, u32[]{:S(2)}) collective-permute-start(bf16[5248,128]{1,0:T(8,128)(2,1)S(1)} %get-tuple-element.83), channel_id=1, source_target_pairs={{8,0},{16,8},{24,16},{32,24},{40,32},{48,40},{56,48},{64,56},{72,6... | collective-permute-start | bytes 4030472 | tf_op jit(solution)/shard_map/ppermute | solution.py:47
  20.9 17.5 %sort_half.2 = (bf16[5248,128]{1,0:T(8,128)(2,1)S(1)}, bf16[5248,128]{1,0:T(8,128)(2,1)S(1)}, s32[136,128]{1,0:T(8,128)S(1)}, s32[136,128]{1,0:T(8,128)S(1)}) custom-call(s32[1,1024]{1,0:T(1,128)} %bitcast.22, s32[16,1024]{1,0:T(8,128)} %bitcast.18, s32[16,1024]{1,0:T(8,128)} %bitcast.20, bf16[16384,128]{1,0:T(8,128)(2,1)} %bitcast.14), custom_call_target="tpu_custom_call" | custom-call | flops 1000000000 | bytes 52428800 | tf_op jit(solution)/shard_map/sort_half/pallas_call | solution.py:268
  38.5 0.0 copy-start.4
  38.5 1.9 %collective-permute-start.6 = (bf16[5248,128]{1,0:T(8,128)(2,1)S(1)}, bf16[5248,128]{1,0:T(8,128)(2,1)S(1)}, u32[]{:S(2)}, u32[]{:S(2)}) collective-permute-start(bf16[5248,128]{1,0:T(8,128)(2,1)S(1)} %get-tuple-element.77), channel_id=1, source_target_pairs={{8,0},{16,8},{24,16},{32,24},{40,32},{48,40},{56,48},{64,56},{72,6... | collective-permute-start | bytes 4030472 | tf_op jit(solution)/shard_map/ppermute | solution.py:47
  40.4 1.9 %collective-permute-start.9 = (s32[136,128]{1,0:T(8,128)S(1)}, s32[136,128]{1,0:T(8,128)S(1)}, u32[]{:S(2)}, u32[]{:S(2)}) collective-permute-start(s32[136,128]{1,0:T(8,128)S(1)} %get-tuple-element.84), channel_id=1, source_target_pairs={{8,0},{16,8},{24,16},{32,24},{40,32},{48,40},{56,48},{64,56},{72,6... | collective-permute-start | bytes 208904 | tf_op jit(solution)/shard_map/ppermute | solution.py:47
  42.3 1.9 %collective-permute-start.7 = (s32[136,128]{1,0:T(8,128)S(1)}, s32[136,128]{1,0:T(8,128)S(1)}, u32[]{:S(2)}, u32[]{:S(2)}) collective-permute-start(s32[136,128]{1,0:T(8,128)S(1)} %get-tuple-element.78), channel_id=1, source_target_pairs={{8,0},{16,8},{24,16},{32,24},{40,32},{48,40},{56,48},{64,56},{72,6... | collective-permute-start | bytes 208904 | tf_op jit(solution)/shard_map/ppermute | solution.py:47
  44.3 0.0 copy-done.13
  44.3 0.0 copy-done.12
  44.3 0.6 pad_maximum_fusion.1.obs_ref
  44.9 0.0 copy-done.3
  44.9 0.0 copy-start.9
  44.9 0.0 copy-start.10
  44.9 0.0 copy-start.11
  44.9 9.3 %predict.3.refs_4_ = f32[8,128]{1,0:T(8,128)S(1)} custom-call(bf16[240,8192]{1,0:T(8,128)(2,1)S(1)} %copy-done.3, bf16[5248,128]{1,0:T(8,128)(2,1)S(1)} %get-tuple-element.79.refs_1_, bf16[5248,128]{1,0:T(8,128)(2,1)S(1)} %get-tuple-element.80.refs_2_, s32[136,128]{1,0:T(8,128)S(1)} %get-tuple-element.81.refs_3_.refs_5_.refs_6_, ...), custom_call_target="tpu_custom_call" | custom-call | flops 1006632960 | bytes 20971520 | tf_op jit(solution)/shard_map/predict/pallas_call | solution.py:340
  54.2 5.8 %collective-permute-done.9.refs_2_.refs_3_ = s32[136,128]{1,0:T(8,128)S(1)} collective-permute-done((s32[136,128]{1,0:T(8,128)S(1)}, s32[136,128]{1,0:T(8,128)S(1)}, u32[]{:S(2)}, u32[]{:S(2)}) %collective-permute-start.9) | collective-permute-done | bytes 69664 | tf_op jit(solution)/shard_map/ppermute | solution.py:47
  60.0 0.0 collective-permute-done.8.refs_1_
  60.0 6.7 %predict.4.refs_5_ = f32[8,128]{1,0:T(8,128)S(1)} custom-call(bf16[240,8192]{1,0:T(8,128)(2,1)S(1)} %copy-done.3, bf16[5248,128]{1,0:T(8,128)(2,1)S(1)} %collective-permute-done.8.refs_1_, s32[136,128]{1,0:T(8,128)S(1)} %collective-permute-done.9.refs_2_.refs_3_, s32[136,128]{1,0:T(8,128)S(1)} %collective-permute-done.9.refs_2_.refs_3_), custom_call_target="tpu_custom_call" | custom-call | flops 503316480 | bytes 15728640 | tf_op jit(solution)/shard_map/predict/pallas_call | solution.py:340
  66.7 0.0 collective-permute-done.7.refs_2_.refs_3_
  66.7 0.0 collective-permute-done.6.refs_1_
  66.7 0.0 copy-done.4
  66.7 0.0 copy-start.6
  66.7 1.1 copy-done.6
  67.8 6.7 %predict.5.p_ref = f32[3,8,128]{2,1,0:T(8,128)S(1)} custom-call(bf16[240,8192]{1,0:T(8,128)(2,1)S(1)} %copy-done.3, bf16[5248,128]{1,0:T(8,128)(2,1)S(1)} %collective-permute-done.6.refs_1_, s32[136,128]{1,0:T(8,128)S(1)} %collective-permute-done.7.refs_2_.refs_3_, s32[136,128]{1,0:T(8,128)S(1)} %collective-permute-done.7.refs_2_.refs_3_, ...), custom_call_target="tpu_custom_call" | custom-call | flops 503316480 | bytes 15728640 | tf_op jit(solution)/shard_map/predict/pallas_call | solution.py:340
  74.5 0.0 copy-start.1
  74.5 0.6 copy-done.1
  75.1 19.6 %exchange.1 = (f32[2,8,128]{2,1,0:T(8,128)S(1)}, f32[8,128]{1,0:T(8,128)}) custom-call(f32[3,8,128]{2,1,0:T(8,128)} %copy-done.1, f32[2,8,128]{2,1,0:T(8,128)} %pad_maximum_fusion.1.obs_ref), custom_call_target="tpu_custom_call" | custom-call | tf_op jit(solution)/shard_map/exchange/pallas_call | solution.py:472
  94.7 1.2 slice.21
  96.5 0.0 copy-done.9
  96.6 0.0 copy-done.10
  96.6 0.0 copy-done.11
  96.6 37.5 %conditional.1 = (f32[240,8192]{1,0:T(8,128)}) conditional(s32[]{:T(128)} %bitcast.11, (f32[2,8,128]{2,1,0:T(8,128)S(1)}, f32[240,8192]{1,0:T(8,128)}, bf16[5248,128]{1,0:T(8,128)(2,1)S(1)}, bf16[5248,128]{1,0:T(8,128)(2,1)}, bf16[5248,128]{1,0:T(8,128)(2,1)S(1)}, /*index=5*/bf16[5248,128]{1,0:T(8,128)(2,1)}, s32[136,128]{1,0:T(8,128)S(1)}, ...), branch_computations={%region_0.0_spmd, %region_1.4_spmd} | conditional | flops 6836399616 | bytes 253735552 | solution.py:696
  96.6 0.0 copy-start
  96.6 0.0 copy-start.2
  96.6 0.0 copy-start.5
  96.6 0.0 copy-start.7
  96.6 7.4 %edges.1 = (f32[24,8192]{1,0:T(8,128)S(1)}, f32[24,8192]{1,0:T(8,128)S(1)}) custom-call(f32[2,8,128]{2,1,0:T(8,128)S(1)} %get-tuple-element.46.w_ref, f32[240,8192]{1,0:T(8,128)} %get-tuple-element.47.ps_head.ps_tail.ps_ref, f32[240,8192]{1,0:T(8,128)} %get-tuple-element.47.ps_head.ps_tail.ps_ref, bf16[5248,128]{1,0:T(8,128)(2,1)S(1)} %get-tuple-element.48.refs_0_, ...), custom_call_target="tpu_custom_call" | custom-call | flops 100000000 | bytes 8388608 | tf_op jit(solution)/shard_map/cond/branch_0_fun/edges/pallas_call | solution.py:532
  104.1 2.3 %collective-permute-start.1 = (f32[24,8192]{1,0:T(8,128)S(1)}, f32[24,8192]{1,0:T(8,128)S(1)}, u32[]{:S(2)}, u32[]{:S(2)}) collective-permute-start(f32[24,8192]{1,0:T(8,128)S(1)} %get-tuple-element.56.head_ref), channel_id=1, source_target_pairs={{8,0},{16,8},{24,16},{32,24},{40,32},{48,40},{56,48},{64,56},{72,6... | collective-permute-start | bytes 2359304 | tf_op jit(solution)/shard_map/cond/branch_0_fun/ppermute | solution.py:47
  106.4 4.8 %collective-permute-start = (f32[24,8192]{1,0:T(8,128)S(1)}, f32[24,8192]{1,0:T(8,128)}, u32[]{:S(2)}, u32[]{:S(2)}) collective-permute-start(f32[24,8192]{1,0:T(8,128)S(1)} %get-tuple-element.57.tail_ref), channel_id=1, source_target_pairs={{0,8},{8,16},{16,24},{24,32},{32,40},{40,48},{48,56},{56,64},{64,7... | collective-permute-start | bytes 2359304 | tf_op jit(solution)/shard_map/cond/branch_0_fun/ppermute | solution.py:47
  111.2 0.0 copy-done
  111.2 0.0 copy-done.2
  111.2 0.0 copy-done.5
  111.2 0.0 copy-done.7
  111.2 17.9 %inner.1.own_ref = f32[240,8192]{1,0:T(8,128)} custom-call(f32[2,8,128]{2,1,0:T(8,128)S(1)} %get-tuple-element.46.w_ref, f32[24,8192]{1,0:T(8,128)S(1)} %get-tuple-element.56.head_ref, f32[24,8192]{1,0:T(8,128)S(1)} %get-tuple-element.57.tail_ref, bf16[240,768]{1,0:T(8,128)(2,1)S(1)} %copy-done, f32[240,8192]{1,0:T(8,128)S(1)} %copy-done.2, ...), custom_call_target="tpu_custom_call" | custom-call | flops 4000000000 | bytes 41943040 | tf_op jit(solution)/shard_map/cond/branch_0_fun/inner/pallas_call | solution.py:596
  129.1 0.0 collective-permute-done.1.below_ref
  129.1 0.0 copy-start.8
  129.1 0.9 copy-done.8
  130.0 0.0 collective-permute-done.above_ref
  130.0 3.8 %finish.1 = f32[240,8192]{1,0:T(8,128)} custom-call(f32[240,8192]{1,0:T(8,128)} %inner.1.own_ref, f32[240,8192]{1,0:T(8,128)} %get-tuple-element.47.ps_head.ps_tail.ps_ref, f32[24,8192]{1,0:T(8,128)} %collective-permute-done.above_ref, f32[24,8192]{1,0:T(8,128)} %copy-done.8), custom_call_target="tpu_custom_call", output_to_operand_aliasing={{}: (0, {})} | custom-call | tf_op jit(solution)/shard_map/cond/branch_0_fun/finish/pallas_call | solution.py:650
Async XLA Ops:
  0.0 44.3 %copy-start.13 = (f32[1024]{0:T(1024)S(1)}, f32[1024]{0:T(1024)}, u32[]{:S(2)}) copy-start(f32[1024]{0:T(1024)} %param.14) | copy-start | bytes 12292
  0.0 44.3 %copy-start.12 = (f32[1024]{0:T(1024)S(1)}, f32[1024]{0:T(1024)}, u32[]{:S(2)}) copy-start(f32[1024]{0:T(1024)} %param.15) | copy-start | bytes 12292
  0.0 44.9 %copy-start.3 = (bf16[240,8192]{1,0:T(8,128)(2,1)S(1)}, bf16[240,8192]{1,0:T(8,128)(2,1)}, u32[]{:S(2)}) copy-start(bf16[240,8192]{1,0:T(8,128)(2,1)} %refs_0_.5) | copy-start | bytes 11796484
  17.7 42.4 %collective-permute-start.8 = (bf16[5248,128]{1,0:T(8,128)(2,1)S(1)}, bf16[5248,128]{1,0:T(8,128)(2,1)S(1)}, u32[]{:S(2)}, u32[]{:S(2)}) collective-permute-start(bf16[5248,128]{1,0:T(8,128)(2,1)S(1)} %get-tuple-element.83), channel_id=1, source_target_pairs={{8,0},{16,8},{24,16},{32,24},{40,32},{48,40},{56,48},{64,56},{72,6... | collective-permute-start | bytes 4030472 | tf_op jit(solution)/shard_map/ppermute | solution.py:47
  38.5 28.2 %copy-start.4 = (bf16[5248,128]{1,0:T(8,128)(2,1)}, bf16[5248,128]{1,0:T(8,128)(2,1)S(1)}, u32[]{:S(2)}) copy-start(bf16[5248,128]{1,0:T(8,128)(2,1)S(1)} %get-tuple-element.80.refs_2_) | copy-start | bytes 4030468
  38.5 28.2 %collective-permute-start.6 = (bf16[5248,128]{1,0:T(8,128)(2,1)S(1)}, bf16[5248,128]{1,0:T(8,128)(2,1)S(1)}, u32[]{:S(2)}, u32[]{:S(2)}) collective-permute-start(bf16[5248,128]{1,0:T(8,128)(2,1)S(1)} %get-tuple-element.77), channel_id=1, source_target_pairs={{8,0},{16,8},{24,16},{32,24},{40,32},{48,40},{56,48},{64,56},{72,6... | collective-permute-start | bytes 4030472 | tf_op jit(solution)/shard_map/ppermute | solution.py:47
  40.4 19.6 %collective-permute-start.9 = (s32[136,128]{1,0:T(8,128)S(1)}, s32[136,128]{1,0:T(8,128)S(1)}, u32[]{:S(2)}, u32[]{:S(2)}) collective-permute-start(s32[136,128]{1,0:T(8,128)S(1)} %get-tuple-element.84), channel_id=1, source_target_pairs={{8,0},{16,8},{24,16},{32,24},{40,32},{48,40},{56,48},{64,56},{72,6... | collective-permute-start | bytes 208904 | tf_op jit(solution)/shard_map/ppermute | solution.py:47
  42.3 24.3 %collective-permute-start.7 = (s32[136,128]{1,0:T(8,128)S(1)}, s32[136,128]{1,0:T(8,128)S(1)}, u32[]{:S(2)}, u32[]{:S(2)}) collective-permute-start(s32[136,128]{1,0:T(8,128)S(1)} %get-tuple-element.78), channel_id=1, source_target_pairs={{8,0},{16,8},{24,16},{32,24},{40,32},{48,40},{56,48},{64,56},{72,6... | collective-permute-start | bytes 208904 | tf_op jit(solution)/shard_map/ppermute | solution.py:47
  44.9 51.6 %copy-start.9 = (s32[1024,16]{0,1:T(8,128)S(1)}, s32[1024,16]{0,1:T(8,128)}, u32[]{:S(2)}) copy-start(s32[1024,16]{0,1:T(8,128)} %param.17) | copy-start | bytes 196612
  44.9 51.7 %copy-start.10 = (s32[1024,16]{0,1:T(8,128)S(1)}, s32[1024,16]{0,1:T(8,128)}, u32[]{:S(2)}) copy-start(s32[1024,16]{0,1:T(8,128)} %param.18) | copy-start | bytes 196612
  44.9 51.7 %copy-start.11 = (s32[1024]{0:T(1024)S(1)}, s32[1024]{0:T(1024)}, u32[]{:S(2)}) copy-start(s32[1024]{0:T(1024)} %param.16) | copy-start | bytes 12292
  66.7 1.1 copy-start.6
  74.5 0.6 copy-start.1
  96.6 14.6 %copy-start = (bf16[240,768]{1,0:T(8,128)(2,1)S(1)}, bf16[240,768]{1,0:T(8,128)(2,1)}, u32[]{:S(2)}) copy-start(bf16[240,768]{1,0:T(8,128)(2,1)} %constant.25.clone.1.kern_ref) | copy-start | bytes 1105924 | tf_op jit(solution)/shard_map/cond
  96.6 14.6 %copy-start.2 = (f32[240,8192]{1,0:T(8,128)S(1)}, f32[240,8192]{1,0:T(8,128)}, u32[]{:S(2)}) copy-start(f32[240,8192]{1,0:T(8,128)} %get-tuple-element.47.ps_head.ps_tail.ps_ref) | copy-start | bytes 23592964 | tf_op jit(solution)/shard_map/cond
  96.6 14.6 %copy-start.5 = (bf16[5248,128]{1,0:T(8,128)(2,1)S(1)}, bf16[5248,128]{1,0:T(8,128)(2,1)}, u32[]{:S(2)}) copy-start(bf16[5248,128]{1,0:T(8,128)(2,1)} %get-tuple-element.49.refs_1_) | copy-start | bytes 4030468 | tf_op jit(solution)/shard_map/cond
  96.6 14.6 %copy-start.7 = (bf16[5248,128]{1,0:T(8,128)(2,1)S(1)}, bf16[5248,128]{1,0:T(8,128)(2,1)}, u32[]{:S(2)}) copy-start(bf16[5248,128]{1,0:T(8,128)(2,1)} %get-tuple-element.51.refs_3_) | copy-start | bytes 4030468 | tf_op jit(solution)/shard_map/cond
  104.1 25.0 %collective-permute-start.1 = (f32[24,8192]{1,0:T(8,128)S(1)}, f32[24,8192]{1,0:T(8,128)S(1)}, u32[]{:S(2)}, u32[]{:S(2)}) collective-permute-start(f32[24,8192]{1,0:T(8,128)S(1)} %get-tuple-element.56.head_ref), channel_id=1, source_target_pairs={{8,0},{16,8},{24,16},{32,24},{40,32},{48,40},{56,48},{64,56},{72,6... | collective-permute-start | bytes 2359304 | tf_op jit(solution)/shard_map/cond/branch_0_fun/ppermute | solution.py:47
  106.4 23.6 %collective-permute-start = (f32[24,8192]{1,0:T(8,128)S(1)}, f32[24,8192]{1,0:T(8,128)}, u32[]{:S(2)}, u32[]{:S(2)}) collective-permute-start(f32[24,8192]{1,0:T(8,128)S(1)} %get-tuple-element.57.tail_ref), channel_id=1, source_target_pairs={{0,8},{8,16},{16,24},{24,32},{32,40},{40,48},{48,56},{56,64},{64,7... | collective-permute-start | bytes 2359304 | tf_op jit(solution)/shard_map/cond/branch_0_fun/ppermute | solution.py:47
  129.1 0.9 copy-start.8
